TPU v7x, 256 devices: a whole 4x4x8 slice. The times are simulated.
256 devices in a mesh: slab: 8 (over y, core), wall: 32 (over x, z).
Axes of the slice: x: 4, y: 4, z: 8, core: 2. Of those that a mesh axis runs over, the one named last changes fastest.
Arguments:
- flow_state: float32 [64, 5, 262144], P(None, None, ('slab', 'wall')), as said below
- match_elem: int32 [2097152], P(('slab', 'wall')), may hold values from 0 to 1023
- match_coord: int32 [3, 2097152], P(None, ('slab', 'wall')), may hold values from 0 to 15
- match_dest: int32 [2097152, 1], P(('slab', 'wall')), may hold values from 0 to 31; in each aligned block of 8192 rows (0 to 8191, 8192 to 16383, ...) at most 640 rows name the same one
- roughness: float32 [5242880], P(('slab', 'wall')), may hold values from 4 to 30
Outputs:
- rate: float32 [64, 4, 262144], P(None, None, ('slab', 'wall'))
- wall_shear: float32 [2, 5242880], P(None, ('slab', 'wall'))
Inputs may be any that keep to these rules, and one draw needn't show every extreme that they name: `flow_state`: density lies between 0.8 and 1.25 and the pressure 0.4 (energy - |momentum|^2 / (2 density)) between 0.6 and 1.6 at every node. `match_dest`: among the rows of one device no wall index is named by more than 640 rows, and in every draw some device names one wall index exactly 640 times.
All inputs are finite; a program needn't handle non-finite values.
Results may differ from a plain program's by a relative error of at most 0.0003.
Values sent between devices are 32-bit elements; how exact they have to be, the bound alone decides.
No kernel may reach another device: no remote copies, remote signals or barrier semaphores. Data moves between devices by JAX's collectives and lax.ppermute only.
A program may use at most 64 MiB of HBM per device.

v0:
```python
import jax
import jax.numpy as jnp
import numpy as np
from jax import lax
from jax.experimental import pallas as pl
from jax.experimental.pallas import tpu as pltpu
from jax.sharding import PartitionSpec as P

EX = 4
EY = 2
EZ = 128
RES = 16
NEWTON = 8
CAP = 640
N_WALL = 32
M_DEV = 8192

VISCOSITY = 0.05
FOURIER_LAW_ON = 0.07 / 0.288
KARMAN = 0.41
RELAXATION = 0.35
F32 = jnp.float32
BF16 = jnp.bfloat16


def gauss_points():
    return np.array([-1.0, -1.0 / np.sqrt(5.0), 1.0 / np.sqrt(5.0), 1.0])


def derivative_matrix():
    points = gauss_points()
    bary = [
        1.0 / np.prod([points[i] - points[j] for j in range(4) if j != i]) for i in range(4)
    ]
    matrix = np.zeros((4, 4))
    for i in range(4):
        for j in range(4):
            if i != j:
                matrix[i, j] = bary[j] / bary[i] / (points[i] - points[j])
        matrix[i, i] = -np.sum(matrix[i])
    return matrix


D = derivative_matrix()
EVEN0 = float(0.5 * (D[0, 0] + D[0, 3]))
EVEN1 = float(0.5 * (D[1, 0] + D[1, 3]))
ODD00 = float(0.5 * (D[0, 0] - D[0, 3]))
ODD01 = float(0.5 * (D[0, 1] - D[0, 2]))
ODD10 = float(0.5 * (D[1, 0] - D[1, 3]))
ODD11 = float(0.5 * (D[1, 1] - D[1, 2]))


def line_derivative(u0, u1, u2, u3):
    even = (u0 + u3) - (u1 + u2)
    odd0 = u0 - u3
    odd1 = u1 - u2
    half0 = EVEN0 * even
    half1 = EVEN1 * even
    mean0 = ODD00 * odd0 + ODD01 * odd1
    mean1 = ODD10 * odd0 + ODD11 * odd1
    return mean0 + half0, mean1 + half1, mean1 - half1, mean0 - half0


def iota(shape, dim):
    return lax.broadcasted_iota(jnp.int32, shape, dim)


def entropy_of(rho, mx, my, mz, energy):
    inv_rho = 1.0 / rho
    speed_sq = mx * mx + my * my + mz * mz
    pressure = 0.4 * (energy - 0.5 * speed_sq * inv_rho)
    entropy_s = jnp.log(pressure) - 1.4 * jnp.log(rho)
    inv_p = 1.0 / pressure
    leading = (1.4 - entropy_s) / 0.4 - 0.5 * speed_sq * inv_rho * inv_p
    return leading, mx * inv_p, my * inv_p, mz * inv_p, -rho * inv_p


def line_nodes(direction, line):
    outer, inner = line // 4, line % 4
    if direction == 0:
        return [16 * a + 4 * outer + inner for a in range(4)]
    if direction == 1:
        return [16 * outer + 4 * b + inner for b in range(4)]
    return [16 * outer + 4 * inner + c for c in range(4)]


def pack_x(get_lower, get_upper, up_ref, low_ref):
    pair = iota((8, 128), 0) // 2
    for block in range(16):
        upper = pltpu.roll(get_upper(4 * block), 2, 0)
        lower = get_lower(4 * block)
        for i in range(1, 4):
            upper = jnp.where(pair == i, pltpu.roll(get_upper(4 * block + i), (2 + 2 * i) % 8, 0), upper)
            lower = jnp.where(pair == i, pltpu.roll(get_lower(4 * block + i), 2 * i, 0), lower)
        up_ref[pl.ds(8 * block, 8), :] = upper
        low_ref[pl.ds(8 * block, 8), :] = lower


def pack_z(get_lower, get_upper, up_ref, low_ref):
    lane = iota((8, 128), 1)
    upper = jnp.zeros((8, 128), F32)
    lower = jnp.zeros((8, 128), F32)
    for k in range(64):
        upper = jnp.where(lane == k, pltpu.roll(get_upper(k), (k + 1) % 128, 1), upper)
        low = get_lower(k)
        lower = jnp.where(lane == k, low if k == 0 else pltpu.roll(low, k, 1), lower)
    up_ref[...] = upper
    low_ref[...] = lower


def entropy_kernel(flow_ref, v_ref, xup_ref, xlow_ref, zup_ref, zlow_ref):
    for n in range(64):
        tile, sub = n // 8, n % 8
        state = [flow_ref[pl.ds(c * 512 + tile * 64 + sub, 8, stride=8), :] for c in range(5)]
        values = entropy_of(*state)
        for k in range(4):
            v_ref[k * 64 + n] = values[1 + k]

    def face(direction, end):
        return lambda k: v_ref[(k // 16) * 64 + line_nodes(direction, k % 16)[end]]

    pack_x(face(0, 0), face(0, 3), xup_ref, xlow_ref)
    pack_z(face(2, 0), face(2, 3), zup_ref, zlow_ref)


def flux_kernel(v_ref, xprev_ref, xnext_ref, zprev_ref, znext_ref,
                rate_ref, xup_ref, xlow_ref, zup_ref, zlow_ref, g_ref, f_ref):
    row = iota((8, 128), 0)
    lane = iota((8, 128), 1)
    odd = row % 2 == 1

    def jumps_y(lower, upper):
        prev = jnp.where(odd, pltpu.roll(upper, 1, 0), lower)
        following = jnp.where(odd, upper, pltpu.roll(lower, 7, 0))
        return prev, following

    for k in range(64):
        comp, line = k // 16, k % 16
        for direction in range(3):
            nodes = line_nodes(direction, line)
            u = [v_ref[comp * 64 + n] for n in nodes]
            d = list(line_derivative(*u))
            if direction == 0:
                i = k % 4
                prev_halo = xprev_ref[pl.ds(8 * (k // 4), 8), :]
                next_halo = xnext_ref[pl.ds(8 * (k // 4), 8), :]
                if i:
                    prev_halo = pltpu.roll(prev_halo, 8 - 2 * i, 0)
                if i != 3:
                    next_halo = pltpu.roll(next_halo, 6 - 2 * i, 0)
                prev = jnp.where(row < 2, prev_halo, pltpu.roll(u[3], 2, 0))
                following = jnp.where(row >= 6, next_halo, pltpu.roll(u[0], 6, 0))
            elif direction == 1:
                prev, following = jumps_y(u[0], u[3])
            else:
                prev_halo = zprev_ref[...]
                if k:
                    prev_halo = pltpu.roll(prev_halo, 128 - k, 1)
                next_halo = pltpu.roll(znext_ref[...], 127 - k, 1)
                prev = jnp.where(lane == 0, prev_halo, pltpu.roll(u[3], 1, 1))
                following = jnp.where(lane == 127, next_halo, pltpu.roll(u[0], 127, 1))
            d[0] = d[0] - 3.0 * (prev - u[0])
            d[3] = d[3] + 3.0 * (following - u[3])
            for end in range(4):
                g_ref[(direction * 4 + comp) * 64 + nodes[end]] = d[end]

    def pointwise(n, carry):
        v = [v_ref[c * 64 + n] for c in range(4)]
        g = [[g_ref[(d * 4 + c) * 64 + n] for c in range(4)] for d in range(3)]
        temperature = -1.0 / v[3]
        u = [v[i] * temperature for i in range(3)]
        scaled = VISCOSITY * temperature
        gu = [[scaled * (g[d][i] + u[i] * g[d][3]) for i in range(3)] for d in range(3)]
        third = (2.0 / 3.0) * (gu[0][0] + gu[1][1] + gu[2][2])
        conduct = FOURIER_LAW_ON * temperature * temperature
        tau = [[None] * 3 for _ in range(3)]
        for d in range(3):
            for i in range(d, 3):
                entry = gu[d][i] + gu[i][d]
                if i == d:
                    entry = entry - third
                tau[d][i] = entry
                tau[i][d] = entry
        for d in range(3):
            heat = u[0] * tau[d][0] + u[1] * tau[d][1] + u[2] * tau[d][2] + conduct * g[d][3]
            for c in range(3):
                f_ref[(d * 4 + c) * 64 + n] = tau[d][c]
            f_ref[(d * 4 + 3) * 64 + n] = heat
        return carry

    lax.fori_loop(0, 64, pointwise, 0, unroll=4)

    def face(direction, end):
        return lambda k: f_ref[(direction * 4 + k // 16) * 64 + line_nodes(direction, k % 16)[end]]

    pack_x(face(0, 0), face(0, 3), xup_ref, xlow_ref)
    pack_z(face(2, 0), face(2, 3), zup_ref, zlow_ref)

    for direction in range(3):
        for k in range(64):
            comp, line = k // 16, k % 16
            nodes = line_nodes(direction, line)
            u = [f_ref[(direction * 4 + comp) * 64 + n] for n in nodes]
            d = list(line_derivative(*u))
            if direction == 0:
                prev = jnp.where(row < 2, 0.0, pltpu.roll(u[3], 2, 0))
                following = jnp.where(row >= 6, 0.0, pltpu.roll(u[0], 6, 0))
            elif direction == 1:
                prev, following = jumps_y(u[0], u[3])
            else:
                prev = jnp.where(lane == 0, 0.0, pltpu.roll(u[3], 1, 1))
                following = jnp.where(lane == 127, 0.0, pltpu.roll(u[0], 127, 1))
            d[0] = d[0] - 3.0 * (prev - u[0])
            d[3] = d[3] + 3.0 * (following - u[3])
            if direction == 1 and comp in (0, 2):
                d[0] = d[0] + jnp.where(odd, 0.0, 6.0 * u[0])
            for end in range(4):
                where = comp * 64 + nodes[end]
                if direction == 0:
                    rate_ref[where] = d[end]
                else:
                    rate_ref[where] = rate_ref[where] + d[end]


def rate_kernel(part_ref, xprev_ref, xnext_ref, zprev_ref, znext_ref, shear_ref, rate_ref):
    row = iota((8, 128), 0)
    lane = iota((8, 128), 1)
    for n in range(64):
        a, b, c = n // 16, n // 4 % 4, n % 4
        for comp in range(4):
            total = part_ref[comp * 64 + n]
            if a in (0, 3):
                k = comp * 16 + 4 * b + c
                i = k % 4
                halo = (xprev_ref if a == 0 else xnext_ref)[pl.ds(8 * (k // 4), 8), :]
                shift = (8 - 2 * i) % 8 if a == 0 else 6 - 2 * i
                if shift:
                    halo = pltpu.roll(halo, shift, 0)
                if a == 0:
                    total = total - jnp.where(row < 2, 3.0 * halo, 0.0)
                else:
                    total = total + jnp.where(row >= 6, 3.0 * halo, 0.0)
            if c in (0, 3):
                k = comp * 16 + 4 * a + b
                halo = (zprev_ref if c == 0 else znext_ref)[...]
                shift = (128 - k) % 128 if c == 0 else 127 - k
                if shift:
                    halo = pltpu.roll(halo, shift, 1)
                if c == 0:
                    total = total - jnp.where(lane == 0, 3.0 * halo, 0.0)
                else:
                    total = total + jnp.where(lane == 127, 3.0 * halo, 0.0)
            if b == 0 and comp in (0, 2):
                total = total - 6.0 * shear_ref[(comp // 2) * 16 + 4 * a + c]
            rate_ref[pl.ds(n * 32 + comp, 8, stride=4), :] = total


PROBE_BLOCK = 512


def probe_kernel(flow_ref, elem_ref, coord_ref, dest_ref, probe_ref, rank_ref, lhs_ref):
    points = gauss_points()
    for part, comp in enumerate((0, 1, 3)):
        value = flow_ref[comp]
        high = value.astype(BF16)
        lhs_ref[pl.ds(64 * part, 64), :] = high
        lhs_ref[pl.ds(192 + 64 * part, 64), :] = (value - high.astype(F32)).astype(BF16)

    before = (iota((128, 128), 0) < iota((128, 128), 1)).astype(F32).astype(BF16)
    counter = jnp.concatenate([before, jnp.ones((128, 128), BF16)], axis=1)
    wall_ids = iota((N_WALL, 128), 0)

    def rank_block(block, total):
        dest = dest_ref[0:1, pl.ds(pl.multiple_of(block * 128, 128), 128)]
        hot = (wall_ids == dest).astype(F32)
        counts = jnp.dot(hot.astype(BF16), counter, preferred_element_type=F32)
        rank = jnp.sum(hot * (counts[:, :128] + total), axis=0, keepdims=True)
        rank_ref[pl.ds(block, 1), :] = rank.astype(jnp.int32)
        return total + counts[:, 128:]

    lax.fori_loop(0, M_DEV // 128, rank_block, jnp.zeros((N_WALL, 128), F32), unroll=4)

    def basis_rows(coordinate, index):
        product = jnp.ones_like(coordinate)
        scale = 1.0
        for other in range(4):
            node = float(points[other])
            product = product * jnp.where(index == other, 1.0, coordinate - node)
        scales = [
            float(1.0 / np.prod([points[i] - points[j] for j in range(4) if j != i])) for i in range(4)
        ]
        scale = jnp.where(
            index == 0, scales[0], jnp.where(index == 1, scales[1], jnp.where(index == 2, scales[2], scales[3]))
        )
        return product * scale

    width = PROBE_BLOCK
    elem_ids = iota((1024, width), 0)
    row16 = iota((16, width), 0)

    def probe_block(block, carry):
        start = pl.multiple_of(block * width, width)
        elem = elem_ref[0:1, pl.ds(start, width)]
        hot = (elem_ids == elem).astype(F32).astype(BF16)
        picked = jnp.dot(lhs_ref[...], hot, preferred_element_type=F32)
        coords = [
            (2.0 * coord_ref[d : d + 1, pl.ds(start, width)].astype(F32) + 1.0) / RES - 1.0 for d in range(3)
        ]
        wide = [jnp.broadcast_to(coords[d], (16, width)) for d in range(3)]
        along_yz = basis_rows(wide[1], row16 // 4) * basis_rows(wide[2], row16 % 4)
        along_x = [basis_rows(wide[0], jnp.full((16, width), a, jnp.int32)) for a in range(4)]
        for part in range(3):
            total = None
            for a in range(4):
                base = 64 * part + 16 * a
                term = along_x[a] * (picked[base : base + 16] + picked[192 + base : 192 + base + 16])
                total = term if total is None else total + term
            value = jnp.sum(total * along_yz, axis=0, keepdims=True)
            for i in range(width // 128):
                probe_ref[part, pl.ds(block * (width // 128) + i, 1), :] = value[:, 128 * i : 128 * (i + 1)]
        layer = (elem // EZ % EY).astype(F32)
        height = 2.0 * layer + 1.0 + coords[1]
        for i in range(width // 128):
            probe_ref[3, pl.ds(block * (width // 128) + i, 1), :] = height[:, 128 * i : 128 * (i + 1)]
        return carry

    lax.fori_loop(0, M_DEV // width, probe_block, 0)


def wall_model(mass_per_volume, mom_x, mom_z, height, factor):
    vel_x = mom_x / mass_per_volume
    vel_z = mom_z / mass_per_volume
    slip_speed = jnp.maximum(jnp.sqrt(vel_x * vel_x + vel_z * vel_z), 0.5)
    reynolds = height * slip_speed * mass_per_volume / VISCOSITY
    log_term = jnp.log(factor * reynolds)
    newton_ratio = jnp.ones_like(mass_per_volume)
    for sweep_index in range(NEWTON):
        residue = newton_ratio - (log_term - jnp.log(newton_ratio)) / KARMAN
        newton_slope = 1.0 + 1.0 / (KARMAN * newton_ratio)
        newton_ratio = newton_ratio - RELAXATION * residue / newton_slope
    friction = slip_speed / newton_ratio
    stress_scale = mass_per_volume * friction * friction / slip_speed
    return (stress_scale * vel_x, stress_scale * vel_z)


WALL_BLOCK = 1024


def wall_kernel(probe_ref, rank_ref, dest_ref, rough_ref, slots_ref, shear_ref, lhs_ref, hot_ref):
    rows = M_DEV // 128
    rank = rank_ref[...]
    dest = dest_ref[...]
    lane = rank % 128
    table_row = dest * (CAP // 128) + rank // 128

    def pick(r, total):
        entry = jnp.broadcast_to(rough_ref[pl.ds(r, 1), :], (rows, 128))
        entry = jnp.take_along_axis(entry, lane, axis=1, mode="promise_in_bounds")
        return jnp.where(table_row == r, entry, total)

    factor = lax.fori_loop(0, CAP * N_WALL // 128, pick, jnp.ones((rows, 128), F32), unroll=4)
    shear = wall_model(probe_ref[0], probe_ref[1], probe_ref[2], probe_ref[3], factor)

    shear_ref[...] = jnp.zeros_like(shear_ref)
    parts = []
    for comp in range(2):
        for pair in range(16):
            shear_ref[pl.ds(128 * comp + 8 * pair, 4, stride=2), :] = shear[comp][4 * pair : 4 * pair + 4]
        high = shear[comp].astype(BF16).astype(F32)
        parts += [high, shear[comp] - high]

    code = (rank // 256) * N_WALL + dest
    low = rank % 256
    code_ids = iota((96, 128), 0)
    low_ids = iota((256, 128), 0)
    total = jnp.zeros((384, 256), F32)
    per = WALL_BLOCK // 128
    for block in range(M_DEV // WALL_BLOCK):
        for i in range(per):
            r = block * per + i
            match = code_ids == code[r : r + 1]
            for part in range(4):
                lhs_ref[pl.ds(96 * part, 96), pl.ds(128 * r, 128)] = jnp.where(
                    match, parts[part][r : r + 1], 0.0
                ).astype(BF16)
            hot_ref[:, pl.ds(128 * r, 128)] = (low_ids == low[r : r + 1]).astype(F32).astype(BF16)
        span = pl.ds(block * WALL_BLOCK, WALL_BLOCK)
        total = total + lax.dot_general(
            lhs_ref[:, span], hot_ref[:, span], (((1,), (1,)), ((), ())), preferred_element_type=F32
        )
    for comp in range(2):
        both = total[192 * comp : 192 * comp + 96] + total[192 * comp + 96 : 192 * comp + 192]
        for chunk in range(CAP // 128):
            q, half = chunk // 2, chunk % 2
            for w in range(0, N_WALL, 8):
                slots_ref[pl.ds(w * 10 + chunk * 2 + comp, 8, stride=10), :] = both[
                    q * N_WALL + w : q * N_WALL + w + 8, 128 * half : 128 * half + 128
                ]


VMEM = pl.BlockSpec(memory_space=pltpu.VMEM)


def call(kernel, inputs, outputs, scratch=(), name=None):
    return pl.pallas_call(
        kernel,
        out_shape=[jax.ShapeDtypeStruct(shape, dtype) for shape, dtype in outputs],
        in_specs=[VMEM] * len(inputs),
        out_specs=[VMEM] * len(outputs),
        scratch_shapes=[pltpu.VMEM(shape, dtype) for shape, dtype in scratch],
        name=name,
        compiler_params=pltpu.CompilerParams(vmem_limit_bytes=40 * 1024 * 1024),
    )(*inputs)


def ring(axis, step):
    count = lax.axis_size(axis)
    return [(i, (i + step) % count) for i in range(count)]


def exchange(xup, xlow, zup, zlow):
    return (
        lax.ppermute(xup, "slab", ring("slab", 1)),
        lax.ppermute(xlow, "slab", ring("slab", -1)),
        lax.ppermute(zup, "wall", ring("wall", 1)),
        lax.ppermute(zlow, "wall", ring("wall", -1)),
    )


def local(flow_state, match_elem, match_coord, match_dest, roughness):
    faces = [((128, 128), F32), ((128, 128), F32), ((8, 128), F32), ((8, 128), F32)]
    flow = flow_state.transpose(1, 0, 2)
    flow_rows = flow.reshape(5, 8, 8, 8, 128).transpose(0, 1, 3, 2, 4).reshape(2560, 128)
    rough = lax.all_to_all(roughness.reshape(N_WALL, 1, CAP), "wall", 0, 0, tiled=True).reshape(160, 128)
    v, *packs = call(entropy_kernel, [flow_rows], [((256, 8, 128), F32)] + faces, name="entropy")
    halos = exchange(*packs)
    probe, rank = call(
        probe_kernel,
        [flow, match_elem.reshape(1, M_DEV), match_coord, match_dest.reshape(1, M_DEV)],
        [((4, 64, 128), F32), ((64, 128), jnp.int32)],
        [((384, 1024), BF16)],
        name="matching",
    )
    part, *packs = call(
        flux_kernel,
        [v, *halos],
        [((256, 8, 128), F32)] + faces,
        [((768, 8, 128), F32), ((768, 8, 128), F32)],
        name="flux",
    )
    halos = exchange(*packs)
    slots, shear = call(
        wall_kernel,
        [probe, rank, match_dest.reshape(64, 128), rough],
        [((320, 128), F32), ((256, 128), F32)],
        [((384, M_DEV), BF16), ((256, M_DEV), BF16)],
        name="wallmodel",
    )
    outgoing = slots.reshape(N_WALL, 5, 2, 128).transpose(2, 0, 1, 3).reshape(2, N_WALL * CAP)
    wall_shear = lax.all_to_all(outgoing, "wall", split_axis=1, concat_axis=1, tiled=True)
    (rate,) = call(
        rate_kernel, [part, *halos, shear.reshape(32, 8, 128)], [((2048, 128), F32)], name="rate"
    )
    rate = rate.reshape(64, 8, 4, 128).transpose(0, 2, 1, 3).reshape(64, 4, 1024)
    return (rate, wall_shear)


def solution(mesh):
    return jax.shard_map(
        local,
        mesh=mesh,
        in_specs=(
            P(None, None, ("slab", "wall")),
            P(("slab", "wall")),
            P(None, ("slab", "wall")),
            P(("slab", "wall"), None),
            P(("slab", "wall")),
        ),
        out_specs=(P(None, None, ("slab", "wall")), P(None, ("slab", "wall"))),
        check_vma=False,
    )
```

profile of v0, /device:TPU:8, one launch (start us, length us, event | category | flops | bytes accessed | tf_op | source)
XLA Modules:
  0.0 71.8 jit_solution(17869482261973098984)
XLA Ops:
  0.6 11.3 %all-to-all-start = ((f32[32,1,640]{2,1,0:T(1,128)}), f32[32,1,640]{2,1,0:T(1,128)S(1)}, u32[]{:S(2)}, u32[]{:S(2)}) async-start(f32[32,1,640]{2,1,0:T(1,128)} %bitcast.34), calls=%async_computation | async-start | bytes 163840 | tf_op jit(solution)/shard_map/all_to_all | solution.py:434
  12.0 0.0 copy-start
  12.0 1.3 %copy-done = f32[64,5,1024]{2,0,1:T(8,128)S(1)} copy-done((f32[64,5,1024]{2,0,1:T(8,128)S(1)}, f32[64,5,1024]{2,0,1:T(8,128)}, u32[]{:S(2)}) %copy-start) | copy-done | bytes 1310744
  13.3 0.9 %copy-done.2 = s32[3,8192]{1,0:T(4,128)S(1)} copy-done((s32[3,8192]{1,0:T(4,128)S(1)}, s32[3,8192]{1,0:T(4,128)}, u32[]{:S(2)}) %copy-start.2) | copy-done | bytes 98328
  14.2 0.8 %copy-done.3 = s32[8192,1]{0,1:T(1,128)S(1)} copy-done((s32[8192,1]{0,1:T(1,128)S(1)}, s32[8192,1]{0,1:T(1,128)}, u32[]{:S(2)}) %copy-start.3) | copy-done | bytes 32792
  15.0 0.8 %copy-done.5 = s32[8192]{0:T(1024)S(1)} copy-done((s32[8192]{0:T(1024)S(1)}, s32[8192]{0:T(1024)}, u32[]{:S(2)}) %copy-start.5) | copy-done | bytes 32792
  15.7 12.5 %matching.1 = (f32[4,64,128]{2,1,0:T(8,128)S(1)}, s32[64,128]{1,0:T(8,128)S(1)}) custom-call(f32[5,64,1024]{2,1,0:T(8,128)S(1)} %bitcast.23, s32[1,8192]{1,0:T(1,128)S(1)} %bitcast.30, s32[3,8192]{1,0:T(4,128)S(1)} %copy-done.2, s32[1,8192]{1,0:T(1,128)S(1)} %bitcast.28), custom_call_target="tpu_custom_call" | custom-call | tf_op jit(solution)/shard_map/matching/pallas_call | solution.py:405
  28.2 0.0 all-to-all-done
  28.2 10.6 %wallmodel.1 = (f32[320,128]{1,0:T(8,128)S(1)}, f32[256,128]{1,0:T(8,128)S(1)}) custom-call(f32[4,64,128]{2,1,0:T(8,128)S(1)} %get-tuple-element.26.probe_ref, s32[64,128]{1,0:T(8,128)S(1)} %get-tuple-element.27.rank_ref, s32[64,128]{1,0:T(8,128)S(1)} %bitcast.29, f32[160,128]{1,0:T(8,128)S(1)} %bitcast.25), custom_call_target="tpu_custom_call" | custom-call | tf_op jit(solution)/shard_map/wallmodel/pallas_call | solution.py:405
  39.0 0.8 %copy.12 = f32[2,32,640]{2,0,1:T(2,128)} copy(f32[2,32,640]{2,1,0:T(8,128)S(1)} %all_to_all.12) | data formatting | bytes 327680 | tf_op jit(solution)/shard_map/all_to_all | solution.py:460
  39.8 9.8 %all-to-all-start.1 = ((f32[2,32,640]{2,0,1:T(2,128)}), f32[2,32,640]{2,0,1:T(2,128)S(1)}, u32[]{:S(2)}, u32[]{:S(2)}) async-start(f32[2,32,640]{2,0,1:T(2,128)} %copy.12), calls=%async_computation.1 | async-start | bytes 327680 | tf_op jit(solution)/shard_map/all_to_all | solution.py:460
  49.6 0.4 entropy.1
  50.0 0.0 collective-permute-start
  50.0 1.7 %collective-permute-start.1 = (f32[128,128]{1,0:T(8,128)S(1)}, f32[128,128]{1,0:T(8,128)S(1)}, u32[]{:S(2)}, u32[]{:S(2)}) collective-permute-start(f32[128,128]{1,0:T(8,128)S(1)} %get-tuple-element.18), channel_id=1, source_target_pairs={{0,224},{32,0},{64,32},{96,64},{128,96},{160,128},{192,160},{224,1... | collective-permute-start | bytes 196616 | tf_op jit(solution)/shard_map/ppermute | solution.py:424
  51.7 1.8 %collective-permute-start.2 = (f32[8,128]{1,0:T(8,128)S(1)}, f32[8,128]{1,0:T(8,128)S(1)}, u32[]{:S(2)}, u32[]{:S(2)}) collective-permute-start(f32[8,128]{1,0:T(8,128)S(1)} %get-tuple-element.19), channel_id=1, source_target_pairs={{0,1},{1,2},{2,3},{3,4},{4,5},{5,6},{6,7},{7,8},{8,9},{9,10},{10,1... | collective-permute-start | bytes 12296 | tf_op jit(solution)/shard_map/ppermute | solution.py:425
  53.5 3.6 %collective-permute-start.3 = (f32[8,128]{1,0:T(8,128)S(1)}, f32[8,128]{1,0:T(8,128)S(1)}, u32[]{:S(2)}, u32[]{:S(2)}) collective-permute-start(f32[8,128]{1,0:T(8,128)S(1)} %get-tuple-element.20), channel_id=1, source_target_pairs={{0,31},{1,0},{2,1},{3,2},{4,3},{5,4},{6,5},{7,6},{8,7},{9,8},{10,9... | collective-permute-start | bytes 12296 | tf_op jit(solution)/shard_map/ppermute | solution.py:426
  57.1 1.7 %collective-permute-done.2.zprev_ref = f32[8,128]{1,0:T(8,128)S(1)} collective-permute-done((f32[8,128]{1,0:T(8,128)S(1)}, f32[8,128]{1,0:T(8,128)S(1)}, u32[]{:S(2)}, u32[]{:S(2)}) %collective-permute-start.2) | collective-permute-done | bytes 4128 | tf_op jit(solution)/shard_map/ppermute | solution.py:425
  58.7 2.4 %flux.1 = (f32[256,8,128]{2,1,0:T(8,128)S(1)}, f32[128,128]{1,0:T(8,128)S(1)}, f32[128,128]{1,0:T(8,128)S(1)}, f32[8,128]{1,0:T(8,128)S(1)}, f32[8,128]{1,0:T(8,128)S(1)}) custom-call(f32[256,8,128]{2,1,0:T(8,128)S(1)} %get-tuple-element.16.v_ref, f32[128,128]{1,0:T(8,128)S(1)} %collective-permute-done.xprev_ref, ...), custom_call_target="tpu_custom_call" | custom-call | tf_op jit(solution)/shard_map/flux/pallas_call | solution.py:405
  61.2 0.0 collective-permute-start.4
  61.2 1.7 %collective-permute-start.5 = (f32[128,128]{1,0:T(8,128)S(1)}, f32[128,128]{1,0:T(8,128)S(1)}, u32[]{:S(2)}, u32[]{:S(2)}) collective-permute-start(f32[128,128]{1,0:T(8,128)S(1)} %get-tuple-element.23), channel_id=1, source_target_pairs={{0,224},{32,0},{64,32},{96,64},{128,96},{160,128},{192,160},{224,1... | collective-permute-start | bytes 196616 | tf_op jit(solution)/shard_map/ppermute | solution.py:424
  63.0 5.3 %collective-permute-start.7 = (f32[8,128]{1,0:T(8,128)S(1)}, f32[8,128]{1,0:T(8,128)S(1)}, u32[]{:S(2)}, u32[]{:S(2)}) collective-permute-start(f32[8,128]{1,0:T(8,128)S(1)} %get-tuple-element.25), channel_id=1, source_target_pairs={{0,31},{1,0},{2,1},{3,2},{4,3},{5,4},{6,5},{7,6},{8,7},{9,8},{10,9... | collective-permute-start | bytes 12296 | tf_op jit(solution)/shard_map/ppermute | solution.py:426
  68.3 1.6 %collective-permute-done.6.zprev_ref = f32[8,128]{1,0:T(8,128)S(1)} collective-permute-done((f32[8,128]{1,0:T(8,128)S(1)}, f32[8,128]{1,0:T(8,128)S(1)}, u32[]{:S(2)}, u32[]{:S(2)}) %collective-permute-start.6) | collective-permute-done | bytes 4128 | tf_op jit(solution)/shard_map/ppermute | solution.py:425
  69.9 1.2 %rate.1 = f32[2048,128]{1,0:T(8,128)} custom-call(f32[256,8,128]{2,1,0:T(8,128)S(1)} %get-tuple-element.21.part_ref, f32[128,128]{1,0:T(8,128)S(1)} %collective-permute-done.4.xprev_ref, f32[128,128]{1,0:T(8,128)S(1)} %collective-permute-done.5.xnext_ref, f32[8,128]{1,0:T(8,128)S(1)} %collective-permute-done.6.zprev_ref, ...), custom_call_target="tpu_custom_call" | custom-call | tf_op jit(solution)/shard_map/rate/pallas_call | solution.py:405
  71.1 0.7 copy.16
  (17 shorter events, 0.1 us)
Async XLA Ops:
  0.6 27.6 %copy-start.4 = (s32[8192,1]{0,1:T(1,128)S(1)}, s32[8192,1]{0,1:T(1,128)}, u32[]{:S(2)}) copy-start(s32[8192,1]{0,1:T(1,128)} %param.8) | copy-start | bytes 98308
  0.6 27.6 %all-to-all-start = ((f32[32,1,640]{2,1,0:T(1,128)}), f32[32,1,640]{2,1,0:T(1,128)S(1)}, u32[]{:S(2)}, u32[]{:S(2)}) async-start(f32[32,1,640]{2,1,0:T(1,128)} %bitcast.34), calls=%async_computation | async-start | bytes 163840 | tf_op jit(solution)/shard_map/all_to_all | solution.py:434
  12.0 1.3 %copy-start = (f32[64,5,1024]{2,0,1:T(8,128)S(1)}, f32[64,5,1024]{2,0,1:T(8,128)}, u32[]{:S(2)}) copy-start(f32[64,5,1024]{2,0,1:T(8,128)} %param.5) | copy-start | bytes 3932164
  13.3 0.9 %copy-start.2 = (s32[3,8192]{1,0:T(4,128)S(1)}, s32[3,8192]{1,0:T(4,128)}, u32[]{:S(2)}) copy-start(s32[3,8192]{1,0:T(4,128)} %coord_ref.1) | copy-start | bytes 294916
  14.2 0.8 %copy-start.3 = (s32[8192,1]{0,1:T(1,128)S(1)}, s32[8192,1]{0,1:T(1,128)}, u32[]{:S(2)}) copy-start(s32[8192,1]{0,1:T(1,128)} %param.8) | copy-start | bytes 98308
  15.0 0.8 %copy-start.5 = (s32[8192]{0:T(1024)S(1)}, s32[8192]{0:T(1024)}, u32[]{:S(2)}) copy-start(s32[8192]{0:T(1024)} %param.6) | copy-start | bytes 98308
  15.7 33.9 %copy-start.1 = (f32[64,5,1024]{2,0,1:T(8,128)S(1)}, f32[64,5,1024]{2,0,1:T(8,128)}, u32[]{:S(2)}) copy-start(f32[64,5,1024]{2,0,1:T(8,128)} %param.5) | copy-start | bytes 3932164
  39.8 31.3 %all-to-all-start.1 = ((f32[2,32,640]{2,0,1:T(2,128)}), f32[2,32,640]{2,0,1:T(2,128)S(1)}, u32[]{:S(2)}, u32[]{:S(2)}) async-start(f32[2,32,640]{2,0,1:T(2,128)} %copy.12), calls=%async_computation.1 | async-start | bytes 327680 | tf_op jit(solution)/shard_map/all_to_all | solution.py:460
  50.0 8.8 %collective-permute-start = (f32[128,128]{1,0:T(8,128)S(1)}, f32[128,128]{1,0:T(8,128)S(1)}, u32[]{:S(2)}, u32[]{:S(2)}) collective-permute-start(f32[128,128]{1,0:T(8,128)S(1)} %get-tuple-element.17), channel_id=1, source_target_pairs={{0,32},{32,64},{64,96},{96,128},{128,160},{160,192},{192,224},{224... | collective-permute-start | bytes 196616 | tf_op jit(solution)/shard_map/ppermute | solution.py:423
  50.0 8.8 %collective-permute-start.1 = (f32[128,128]{1,0:T(8,128)S(1)}, f32[128,128]{1,0:T(8,128)S(1)}, u32[]{:S(2)}, u32[]{:S(2)}) collective-permute-start(f32[128,128]{1,0:T(8,128)S(1)} %get-tuple-element.18), channel_id=1, source_target_pairs={{0,224},{32,0},{64,32},{96,64},{128,96},{160,128},{192,160},{224,1... | collective-permute-start | bytes 196616 | tf_op jit(solution)/shard_map/ppermute | solution.py:424
  51.7 7.0 %collective-permute-start.2 = (f32[8,128]{1,0:T(8,128)S(1)}, f32[8,128]{1,0:T(8,128)S(1)}, u32[]{:S(2)}, u32[]{:S(2)}) collective-permute-start(f32[8,128]{1,0:T(8,128)S(1)} %get-tuple-element.19), channel_id=1, source_target_pairs={{0,1},{1,2},{2,3},{3,4},{4,5},{5,6},{6,7},{7,8},{8,9},{9,10},{10,1... | collective-permute-start | bytes 12296 | tf_op jit(solution)/shard_map/ppermute | solution.py:425
  53.5 5.2 %collective-permute-start.3 = (f32[8,128]{1,0:T(8,128)S(1)}, f32[8,128]{1,0:T(8,128)S(1)}, u32[]{:S(2)}, u32[]{:S(2)}) collective-permute-start(f32[8,128]{1,0:T(8,128)S(1)} %get-tuple-element.20), channel_id=1, source_target_pairs={{0,31},{1,0},{2,1},{3,2},{4,3},{5,4},{6,5},{7,6},{8,7},{9,8},{10,9... | collective-permute-start | bytes 12296 | tf_op jit(solution)/shard_map/ppermute | solution.py:426
  61.2 8.7 %collective-permute-start.4 = (f32[128,128]{1,0:T(8,128)S(1)}, f32[128,128]{1,0:T(8,128)S(1)}, u32[]{:S(2)}, u32[]{:S(2)}) collective-permute-start(f32[128,128]{1,0:T(8,128)S(1)} %get-tuple-element.22), channel_id=1, source_target_pairs={{0,32},{32,64},{64,96},{96,128},{128,160},{160,192},{192,224},{224... | collective-permute-start | bytes 196616 | tf_op jit(solution)/shard_map/ppermute | solution.py:423
  61.2 8.7 %collective-permute-start.5 = (f32[128,128]{1,0:T(8,128)S(1)}, f32[128,128]{1,0:T(8,128)S(1)}, u32[]{:S(2)}, u32[]{:S(2)}) collective-permute-start(f32[128,128]{1,0:T(8,128)S(1)} %get-tuple-element.23), channel_id=1, source_target_pairs={{0,224},{32,0},{64,32},{96,64},{128,96},{160,128},{192,160},{224,1... | collective-permute-start | bytes 196616 | tf_op jit(solution)/shard_map/ppermute | solution.py:424
  63.0 6.9 %collective-permute-start.6 = (f32[8,128]{1,0:T(8,128)S(1)}, f32[8,128]{1,0:T(8,128)S(1)}, u32[]{:S(2)}, u32[]{:S(2)}) collective-permute-start(f32[8,128]{1,0:T(8,128)S(1)} %get-tuple-element.24), channel_id=1, source_target_pairs={{0,1},{1,2},{2,3},{3,4},{4,5},{5,6},{6,7},{7,8},{8,9},{9,10},{10,1... | collective-permute-start | bytes 12296 | tf_op jit(solution)/shard_map/ppermute | solution.py:425
  63.0 6.9 %collective-permute-start.7 = (f32[8,128]{1,0:T(8,128)S(1)}, f32[8,128]{1,0:T(8,128)S(1)}, u32[]{:S(2)}, u32[]{:S(2)}) collective-permute-start(f32[8,128]{1,0:T(8,128)S(1)} %get-tuple-element.25), channel_id=1, source_target_pairs={{0,31},{1,0},{2,1},{3,2},{4,3},{5,4},{6,5},{7,6},{8,7},{9,8},{10,9... | collective-permute-start | bytes 12296 | tf_op jit(solution)/shard_map/ppermute | solution.py:426
where the time goes:
time: 72.9 us; the launch traced here: 71.8 us
  starting transfers between devices  35.3 us (48%)
  Pallas kernels  27.2 us (37%)
  local copies, waits for them, and re-layouts  5.28 us (7%)
  waiting for transfers between devices  3.26 us (4%)
  between operations  0.76 us (1%)
    pallas_call x5, Pallas kernels, call(): pl.pallas_call(kernel, out_shape=[jax.ShapeDtypeStruct(shape, dtype) for...  27.2 us
    all_to_all x1, starting transfers between devices, local(): lax.all_to_all(roughness.reshape(N_WALL, 1, CAP), 'wall', 0, 0, tiled=True)  11.3 us
    all_to_all x1, starting transfers between devices, local(): lax.all_to_all(outgoing, 'wall', split_axis=1, concat_axis=1, tiled=True)  9.78 us
    ppermute x2, starting transfers between devices, exchange(): lax.ppermute(zlow, 'wall', ring('wall', -1))  8.9 us
    unnamed x13, local copies, waits for them, and re-layouts  4.4 us
    ppermute x2, starting transfers between devices, exchange(): lax.ppermute(xlow, 'slab', ring('slab', -1))  3.47 us
    ppermute x2, waiting for transfers between devices, exchange(): lax.ppermute(zup, 'wall', ring('wall', 1))  3.24 us
    ppermute x2, starting transfers between devices, exchange(): lax.ppermute(zup, 'wall', ring('wall', 1))  1.79 us
  transfers between devices with their start and end apart: 10, of which 2 were waited for; matrix products, arithmetic and copies ran while one was open for 0% of the time, Pallas kernels for 23%

commit v1 on v0

v1 whole, which is shorter than its diff:
```python
import jax
import jax.numpy as jnp
import numpy as np
from jax import lax
from jax.experimental import pallas as pl
from jax.experimental.pallas import tpu as pltpu
from jax.sharding import PartitionSpec as P

EX = 4
EY = 2
EZ = 128
RES = 16
NEWTON = 8
CAP = 640
N_WALL = 32
M_DEV = 8192

VISCOSITY = 0.05
FOURIER_LAW_ON = 0.07 / 0.288
KARMAN = 0.41
RELAXATION = 0.35
F32 = jnp.float32
BF16 = jnp.bfloat16


def gauss_points():
    return np.array([-1.0, -1.0 / np.sqrt(5.0), 1.0 / np.sqrt(5.0), 1.0])


def derivative_matrix():
    points = gauss_points()
    bary = [
        1.0 / np.prod([points[i] - points[j] for j in range(4) if j != i]) for i in range(4)
    ]
    matrix = np.zeros((4, 4))
    for i in range(4):
        for j in range(4):
            if i != j:
                matrix[i, j] = bary[j] / bary[i] / (points[i] - points[j])
        matrix[i, i] = -np.sum(matrix[i])
    return matrix


D = derivative_matrix()
EVEN0 = float(0.5 * (D[0, 0] + D[0, 3]))
EVEN1 = float(0.5 * (D[1, 0] + D[1, 3]))
ODD00 = float(0.5 * (D[0, 0] - D[0, 3]))
ODD01 = float(0.5 * (D[0, 1] - D[0, 2]))
ODD10 = float(0.5 * (D[1, 0] - D[1, 3]))
ODD11 = float(0.5 * (D[1, 1] - D[1, 2]))


def line_derivative(u0, u1, u2, u3):
    even = (u0 + u3) - (u1 + u2)
    odd0 = u0 - u3
    odd1 = u1 - u2
    half0 = EVEN0 * even
    half1 = EVEN1 * even
    mean0 = ODD00 * odd0 + ODD01 * odd1
    mean1 = ODD10 * odd0 + ODD11 * odd1
    return mean0 + half0, mean1 + half1, mean1 - half1, mean0 - half0


def iota(shape, dim):
    return lax.broadcasted_iota(jnp.int32, shape, dim)


def entropy_of(rho, mx, my, mz, energy):
    inv_rho = 1.0 / rho
    speed_sq = mx * mx + my * my + mz * mz
    pressure = 0.4 * (energy - 0.5 * speed_sq * inv_rho)
    entropy_s = jnp.log(pressure) - 1.4 * jnp.log(rho)
    inv_p = 1.0 / pressure
    leading = (1.4 - entropy_s) / 0.4 - 0.5 * speed_sq * inv_rho * inv_p
    return leading, mx * inv_p, my * inv_p, mz * inv_p, -rho * inv_p


def line_nodes(direction, line):
    outer, inner = line // 4, line % 4
    if direction == 0:
        return [16 * a + 4 * outer + inner for a in range(4)]
    if direction == 1:
        return [16 * outer + 4 * b + inner for b in range(4)]
    return [16 * outer + 4 * inner + c for c in range(4)]


def is_even(axis):
    return lax.rem(lax.axis_index(axis), 2) == 0


def pick(condition, one, other):
    return lax.select(jnp.broadcast_to(condition, one.shape), one, other)


def pack_x(get_lower, get_upper, first_ref, second_ref):
    even = is_even("slab")
    pair = iota((8, 128), 0) // 2
    for block in range(16):
        upper = pltpu.roll(get_upper(4 * block), 2, 0)
        lower = get_lower(4 * block)
        for i in range(1, 4):
            upper = jnp.where(pair == i, pltpu.roll(get_upper(4 * block + i), (2 + 2 * i) % 8, 0), upper)
            lower = jnp.where(pair == i, pltpu.roll(get_lower(4 * block + i), 2 * i, 0), lower)
        first_ref[pl.ds(8 * block, 8), :] = pick(even, upper, lower)
        second_ref[pl.ds(8 * block, 8), :] = pick(even, lower, upper)


def pack_z(get_lower, get_upper):
    lane = iota((8, 128), 1)
    upper = jnp.zeros((8, 128), F32)
    lower = jnp.zeros((8, 128), F32)
    for k in range(64):
        upper = jnp.where(lane == k, pltpu.roll(get_upper(k), (k + 1) % 128, 1), upper)
        low = get_lower(k)
        lower = jnp.where(lane == k, low if k == 0 else pltpu.roll(low, k, 1), lower)
    return upper, lower


def x_halos(first_ref, second_ref, block):
    even = is_even("slab")
    first = first_ref[pl.ds(8 * block, 8), :]
    second = second_ref[pl.ds(8 * block, 8), :]
    return pick(even, second, first), pick(even, first, second)


def entropy_kernel(flow_ref, v_ref, table_ref, x1_ref, x2_ref, z1_ref, z2_ref, rows_ref, sems):
    copies = [
        pltpu.make_async_copy(
            flow_ref.at[:, pl.ds(128 * part, 128), :], rows_ref.at[:, pl.ds(128 * part, 128), :], sems.at[part]
        )
        for part in range(4)
    ]
    for copy in copies:
        copy.start()
    for part in range(4):
        copies[part].wait()
        for n in range(16 * part, 16 * part + 16):
            start = n // 8 * 64 + n % 8
            values = entropy_of(*[rows_ref[c, pl.ds(start, 8, stride=8), :] for c in range(5)])
            for k in range(4):
                v_ref[k * 64 + n] = values[1 + k]
        for field, c in enumerate((0, 1, 3)):
            for j in range(8):
                value = jnp.concatenate(
                    [rows_ref[c, pl.ds(part * 128 + half * 64 + j * 8, 8), :] for half in range(2)], axis=0
                )
                high = value.astype(BF16)
                low = (value - high.astype(F32)).astype(BF16)
                base = j // 2 * 384 + field * 64 + part * 16
                lanes = pl.ds(j % 2 * 128, 128)
                table_ref[pl.ds(base, 16), lanes] = high
                table_ref[pl.ds(base + 192, 16), lanes] = low

    def face(direction, end):
        return lambda k: v_ref[(k // 16) * 64 + line_nodes(direction, k % 16)[end]]

    pack_x(face(0, 0), face(0, 3), x1_ref, x2_ref)
    upper, lower = pack_z(face(2, 0), face(2, 3))
    even = is_even("wall")
    z1_ref[...] = pick(even, upper, lower)
    z2_ref[...] = pick(even, lower, upper)


def jumps_y(lower, upper):
    odd = iota((8, 128), 0) % 2 == 1
    prev = jnp.where(odd, pltpu.roll(upper, 1, 0), lower)
    following = jnp.where(odd, upper, pltpu.roll(lower, 7, 0))
    return prev, following


def flux_kernel(v_ref, x1_ref, x2_ref, z1_ref, z2_ref,
                rate_ref, f1_ref, f2_ref, zup_ref, zlow_ref, g_ref, f_ref):
    row = iota((8, 128), 0)
    lane = iota((8, 128), 1)
    odd = row % 2 == 1
    even = is_even("wall")
    z_prev = pick(even, z2_ref[...], z1_ref[...])
    z_next = pick(even, z1_ref[...], z2_ref[...])

    for k in range(64):
        comp, line = k // 16, k % 16
        for direction in range(3):
            nodes = line_nodes(direction, line)
            u = [v_ref[comp * 64 + n] for n in nodes]
            d = list(line_derivative(*u))
            if direction == 0:
                i = k % 4
                prev_halo, next_halo = x_halos(x1_ref, x2_ref, k // 4)
                if i:
                    prev_halo = pltpu.roll(prev_halo, 8 - 2 * i, 0)
                if i != 3:
                    next_halo = pltpu.roll(next_halo, 6 - 2 * i, 0)
                prev = jnp.where(row < 2, prev_halo, pltpu.roll(u[3], 2, 0))
                following = jnp.where(row >= 6, next_halo, pltpu.roll(u[0], 6, 0))
            elif direction == 1:
                prev, following = jumps_y(u[0], u[3])
            else:
                prev_halo = pltpu.roll(z_prev, 128 - k, 1) if k else z_prev
                next_halo = pltpu.roll(z_next, 127 - k, 1)
                prev = jnp.where(lane == 0, prev_halo, pltpu.roll(u[3], 1, 1))
                following = jnp.where(lane == 127, next_halo, pltpu.roll(u[0], 127, 1))
            d[0] = d[0] - 3.0 * (prev - u[0])
            d[3] = d[3] + 3.0 * (following - u[3])
            for end in range(4):
                g_ref[(direction * 4 + comp) * 64 + nodes[end]] = d[end]

    def pointwise(n, carry):
        v = [v_ref[c * 64 + n] for c in range(4)]
        g = [[g_ref[(d * 4 + c) * 64 + n] for c in range(4)] for d in range(3)]
        temperature = -1.0 / v[3]
        u = [v[i] * temperature for i in range(3)]
        scaled = VISCOSITY * temperature
        gu = [[scaled * (g[d][i] + u[i] * g[d][3]) for i in range(3)] for d in range(3)]
        third = (2.0 / 3.0) * (gu[0][0] + gu[1][1] + gu[2][2])
        conduct = FOURIER_LAW_ON * temperature * temperature
        tau = [[None] * 3 for _ in range(3)]
        for d in range(3):
            for i in range(d, 3):
                entry = gu[d][i] + gu[i][d]
                if i == d:
                    entry = entry - third
                tau[d][i] = entry
                tau[i][d] = entry
        for d in range(3):
            heat = u[0] * tau[d][0] + u[1] * tau[d][1] + u[2] * tau[d][2] + conduct * g[d][3]
            for c in range(3):
                f_ref[(d * 4 + c) * 64 + n] = tau[d][c]
            f_ref[(d * 4 + 3) * 64 + n] = heat
        return carry

    lax.fori_loop(0, 64, pointwise, 0, unroll=4)

    def face(direction, end):
        return lambda k: f_ref[(direction * 4 + k // 16) * 64 + line_nodes(direction, k % 16)[end]]

    pack_x(face(0, 0), face(0, 3), f1_ref, f2_ref)
    zup_ref[...], zlow_ref[...] = pack_z(face(2, 0), face(2, 3))


    for comp in range(4):
        for direction in range(3):
            for line in range(16):
                nodes = line_nodes(direction, line)
                u = [f_ref[(direction * 4 + comp) * 64 + n] for n in nodes]
                d = list(line_derivative(*u))
                if direction == 0:
                    prev = jnp.where(row < 2, 0.0, pltpu.roll(u[3], 2, 0))
                    following = jnp.where(row >= 6, 0.0, pltpu.roll(u[0], 6, 0))
                elif direction == 1:
                    prev, following = jumps_y(u[0], u[3])
                else:
                    prev = jnp.where(lane == 0, 0.0, pltpu.roll(u[3], 1, 1))
                    following = jnp.where(lane == 127, 0.0, pltpu.roll(u[0], 127, 1))
                d[0] = d[0] - 3.0 * (prev - u[0])
                d[3] = d[3] + 3.0 * (following - u[3])
                if direction == 1 and comp in (0, 2):
                    d[0] = d[0] + jnp.where(odd, 0.0, 6.0 * u[0])
                for end in range(4):
                    where = comp * 64 + nodes[end]
                    if direction == 0:
                        rate_ref[where] = d[end]
                    else:
                        rate_ref[where] = rate_ref[where] + d[end]


def rank_kernel(dest_ref, rank_ref, hot_ref, named_ref, count_ref):
    before = (iota((128, 128), 0) < iota((128, 128), 1)).astype(F32).astype(BF16)
    counter = jnp.concatenate([before, jnp.ones((128, 128), BF16)], axis=1)
    wall_ids = iota((N_WALL, 128), 0)
    low_ids = iota((256, 128), 0)
    blocks = M_DEV // 128
    for block in range(blocks):
        named = (wall_ids == dest_ref[0:1, 128 * block : 128 * block + 128]).astype(F32).astype(BF16)
        named_ref[pl.ds(N_WALL * block, N_WALL), :] = named
    count_ref[...] = jnp.dot(named_ref[...], counter, preferred_element_type=F32)
    total = jnp.zeros((N_WALL, 128), F32)
    for block in range(blocks):
        rows = pl.ds(N_WALL * block, N_WALL)
        lanes = pl.ds(128 * block, 128)
        own = wall_ids == dest_ref[0:1, 128 * block : 128 * block + 128]
        rank = jnp.sum(jnp.where(own, count_ref[rows, :128] + total, 0.0), axis=0, keepdims=True).astype(jnp.int32)
        rank_ref[pl.ds(block, 1), :] = rank
        hot_ref[:, lanes] = (low_ids == (rank & 255)).astype(F32).astype(BF16)
        total = total + count_ref[rows, 128:]


PROBE_BLOCK = 256


def probe_kernel(first, last, table_ref, elem_ref, coord_ref, probe_ref):
    points = gauss_points()
    width = PROBE_BLOCK
    scales = [float(1.0 / np.prod([points[i] - points[j] for j in range(4) if j != i])) for i in range(4)]

    def basis_rows(coordinate, index):
        if isinstance(index, int):
            product = scales[index]
            for other in range(4):
                if other != index:
                    product = product * (coordinate - float(points[other]))
            return product
        product = jnp.where(
            index == 0, scales[0], jnp.where(index == 1, scales[1], jnp.where(index == 2, scales[2], scales[3]))
        )
        for other in range(4):
            product = product * jnp.where(index == other, 1.0, coordinate - float(points[other]))
        return product

    low_ids = iota((256, width), 0)
    row16 = iota((16, width), 0)

    def probe_block(block, carry):
        here = pl.ds(pl.multiple_of(block * width, width), width)
        elem = elem_ref[0:1, here]
        hot = (low_ids == elem & 255).astype(F32).astype(BF16)
        picked = jnp.dot(table_ref[...], hot, preferred_element_type=F32).reshape(4, 2, 24, 8, width)
        group = jnp.broadcast_to(elem >> 8, (8, width))
        both = picked[:, 0] + picked[:, 1]
        values = both[0]
        for g in range(1, 4):
            values = jnp.where((group == g)[None], both[g], values)
        values = values.reshape(192, width)
        coords = [(2.0 * coord_ref[d : d + 1, here].astype(F32) + 1.0) / RES - 1.0 for d in range(3)]
        wide = [jnp.broadcast_to(coords[d], (16, width)) for d in range(3)]
        along_yz = basis_rows(wide[1], row16 // 4) * basis_rows(wide[2], row16 % 4)
        along_x = [basis_rows(wide[0], a) for a in range(4)]
        results = []
        for field in range(3):
            total = None
            for a in range(4):
                term = along_x[a] * values[64 * field + 16 * a : 64 * field + 16 * a + 16]
                total = term if total is None else total + term
            results.append(jnp.sum(total * along_yz, axis=0, keepdims=True))
        layer = (elem // EZ % EY).astype(F32)
        results.append(2.0 * layer + 1.0 + coords[1])
        for field in range(4):
            for i in range(width // 128):
                probe_ref[field, pl.ds((block - first) * (width // 128) + i, 1), :] = results[field][
                    :, 128 * i : 128 * (i + 1)
                ]
        return carry

    lax.fori_loop(first, last, probe_block, 0, unroll=4)


SEND_BLOCK = 1024
PER = CAP // 128
CHUNK = 4 * PER + 4


def send_kernel(*refs):
    n_probe = len(refs) - 9
    probe_refs = refs[:n_probe]
    rank_ref, dest_ref, hot_ref, rough_ref, zup_ref, zlow_ref, send_ref, own_ref, lhs_ref = refs[n_probe:]
    rows = M_DEV // 128
    rho, mx, mz, height = [jnp.concatenate([ref[f] for ref in probe_refs], axis=0) for f in range(4)]
    inv_rho = 1.0 / rho
    vel_x = mx * inv_rho
    vel_z = mz * inv_rho
    slip = jnp.maximum(jnp.sqrt(vel_x * vel_x + vel_z * vel_z), 0.5)
    values = [slip * mx, slip * mz, height * slip * rho * (1.0 / VISCOSITY)]
    parts = []
    for f in range(3):
        own_ref[f] = values[f]
        high = values[f].astype(BF16).astype(F32)
        parts += [high, values[f] - high]

    code = (rank_ref[...] // 256) * N_WALL + dest_ref[...]
    code_ids = iota((96, 128), 0)
    total = jnp.zeros((576, 256), F32)
    per = SEND_BLOCK // 128
    for block in range(M_DEV // SEND_BLOCK):
        for i in range(per):
            r = block * per + i
            match = code_ids == code[r : r + 1]
            for part in range(6):
                lhs_ref[pl.ds(96 * part, 96), pl.ds(128 * r, 128)] = jnp.where(
                    match, parts[part][r : r + 1], 0.0
                ).astype(BF16)
        span = pl.ds(block * SEND_BLOCK, SEND_BLOCK)
        total = total + lax.dot_general(
            lhs_ref[:, span], hot_ref[:, span], (((1,), (1,)), ((), ())), preferred_element_type=F32
        )
    for chunk in range(PER):
        q, half = chunk // 2, chunk % 2
        lanes = slice(128 * half, 128 * half + 128)
        for w in range(0, N_WALL, 8):
            for f in range(3):
                base = 192 * f + q * N_WALL + w
                send_ref[pl.ds(w * CHUNK + f * PER + chunk, 8, stride=CHUNK), :] = (
                    total[base : base + 8, lanes] + total[base + 96 : base + 104, lanes]
                )
            send_ref[pl.ds(w * CHUNK + 3 * PER + chunk, 8, stride=CHUNK), :] = rough_ref[
                pl.ds(w * PER + chunk, 8, stride=PER), :
            ]


    half = iota((4, 128), 1) < 64
    upper, lower = [
        jnp.where(half, ref[0:4, :], pltpu.roll(ref[...], 64, 1)[4:8]) for ref in (zup_ref, zlow_ref)
    ]
    target = lax.rem(lax.axis_index("wall") + 1, N_WALL)
    for w in range(N_WALL):
        send_ref[pl.ds(w * CHUNK + 4 * PER, 4), :] = jnp.where(target == w, upper, lower)


def shear_scale(log_term):
    ratio = jnp.ones_like(log_term)
    for sweep in range(NEWTON):
        numerator = KARMAN * ratio - log_term + jnp.log(ratio)
        ratio = ratio - RELAXATION * ratio * numerator / (KARMAN * ratio + 1.0)
    return 1.0 / (ratio * ratio)


def final_kernel(part_ref, x1_ref, x2_ref, got_ref, own_ref, rank_ref, dest_ref, rough_ref,
                 rate_ref, wall_ref, table_ref, factor_ref, shear_ref, out_ref, sems):
    row = iota((8, 128), 0)
    lane = iota((8, 128), 1)
    here = lax.axis_index("wall")
    z_halo = []
    for source in (here + N_WALL - 1, here + 1):
        start = pl.multiple_of(lax.rem(source, N_WALL) * CHUNK + 4 * PER - 4, 8)
        folded = got_ref[pl.ds(start, 8), :]
        unfolded = pltpu.roll(folded, 64, 1)
        z_halo.append(jnp.concatenate([folded[4:8], unfolded[4:8]], axis=0))

    for chunk in range(PER):
        for w in range(0, N_WALL, 16):
            value = jnp.concatenate(
                [got_ref[pl.ds((w + 8 * i) * CHUNK + 3 * PER + chunk, 8, stride=CHUNK), :] for i in range(2)], axis=0
            )
            high = value.astype(BF16)
            table_ref[pl.ds(chunk * N_WALL + w, 16), :128] = high
            table_ref[pl.ds(chunk * N_WALL + w, 16), 128:] = (value - high.astype(F32)).astype(BF16)
    code = (rank_ref[...] >> 7) * N_WALL + dest_ref[...]
    place = rank_ref[...] & 127
    code_ids = iota((PER * N_WALL, 128), 0)
    ids = iota((128, 128), 0)
    for block in range(M_DEV // 512):
        hot = jnp.concatenate(
            [jnp.where(ids == place[r : r + 1], 1.0, 0.0).astype(BF16) for r in range(4 * block, 4 * block + 4)], axis=1
        )
        found = jnp.dot(table_ref[...], jnp.concatenate([hot, hot], axis=0), preferred_element_type=F32)
        for i in range(4):
            r = 4 * block + i
            picked = jnp.where(code_ids == code[r : r + 1], found[:, 128 * i : 128 * i + 128], 0.0)
            factor_ref[pl.ds(r, 1), :] = jnp.sum(picked, axis=0, keepdims=True)
    scale = shear_scale(jnp.log(factor_ref[...] * own_ref[2]))
    shear_ref[...] = jnp.zeros_like(shear_ref)
    for comp in range(2):
        shear = own_ref[comp] * scale
        for pair in range(16):
            shear_ref[pl.ds(128 * comp + 8 * pair, 4, stride=2), :] = shear[4 * pair : 4 * pair + 4]

    for chunk in range(PER):
        for w in range(0, N_WALL, 8):
            vx, vz, reynolds = [
                got_ref[pl.ds(w * CHUNK + f * PER + chunk, 8, stride=CHUNK), :] for f in range(3)
            ]
            used = reynolds > 0.0
            factor = rough_ref[pl.ds(w * PER + chunk, 8, stride=PER), :]
            scale = shear_scale(jnp.log(factor * jnp.where(used, reynolds, 1.0)))
            place = w * PER * 2 + chunk * 2
            wall_ref[pl.ds(place, 8, stride=2 * PER), :] = jnp.where(used, vx * scale, 0.0)
            wall_ref[pl.ds(place + 1, 8, stride=2 * PER), :] = jnp.where(used, vz * scale, 0.0)

    copies = []
    for n in range(64):
        a, b, c = n // 16, n // 4 % 4, n % 4
        for comp in range(4):
            total = part_ref[comp * 64 + n]
            if a in (0, 3):
                k = comp * 16 + 4 * b + c
                i = k % 4
                halo = x_halos(x1_ref, x2_ref, k // 4)[0 if a == 0 else 1]
                shift = (8 - 2 * i) % 8 if a == 0 else 6 - 2 * i
                if shift:
                    halo = pltpu.roll(halo, shift, 0)
                if a == 0:
                    total = total - jnp.where(row < 2, 3.0 * halo, 0.0)
                else:
                    total = total + jnp.where(row >= 6, 3.0 * halo, 0.0)
            if c in (0, 3):
                k = comp * 16 + 4 * a + b
                halo = z_halo[0 if c == 0 else 1]
                shift = (128 - k) % 128 if c == 0 else 127 - k
                if shift:
                    halo = pltpu.roll(halo, shift, 1)
                if c == 0:
                    total = total - jnp.where(lane == 0, 3.0 * halo, 0.0)
                else:
                    total = total + jnp.where(lane == 127, 3.0 * halo, 0.0)
            if b == 0 and comp in (0, 2):
                total = total - 6.0 * shear_ref[pl.ds((comp // 2) * 128 + (4 * a + c) * 8, 8), :]
            out_ref[pl.ds(n * 32 + comp, 8, stride=4), :] = total
        if n % 16 == 15:
            span = pl.ds(512 * a, 512)
            copies.append(pltpu.make_async_copy(out_ref.at[span], rate_ref.at[span], sems.at[a]))
            copies[-1].start()
    for copy in copies:
        copy.wait()


VMEM = pl.BlockSpec(memory_space=pltpu.VMEM)
HBM = pl.BlockSpec(memory_space=pltpu.HBM)


def call(kernel, inputs, outputs, scratch=(), name=None, cost=1, specs=None, out_specs=None, limit=8):
    return pl.pallas_call(
        kernel,
        out_shape=[jax.ShapeDtypeStruct(shape, dtype) for shape, dtype in outputs],
        in_specs=specs or [VMEM] * len(inputs),
        out_specs=out_specs or [VMEM] * len(outputs),
        scratch_shapes=[s if not isinstance(s, tuple) else pltpu.VMEM(*s) for s in scratch],
        name=name,
        cost_estimate=pl.CostEstimate(flops=cost * 10**9, bytes_accessed=cost * 3 * 10**6, transcendentals=0),
        compiler_params=pltpu.CompilerParams(vmem_limit_bytes=int(limit * 1024 * 1024)),
    )(*inputs)


def exchange(axis, first, second, stage):
    count = lax.axis_size(axis)
    with jax.named_scope(stage + "_first"):
        one = lax.ppermute(first, axis, [(i, i + 1 - 2 * (i % 2)) for i in range(count)])
    with jax.named_scope(stage + "_second"):
        other = lax.ppermute(second, axis, [(i, (i - 1 + 2 * (i % 2)) % count) for i in range(count)])
    return one, other


def after(value, *others):
    return lax.optimization_barrier((value, *others))[0]


CUTS = (0, 8, 20, 32)
ENTROPY_LIMIT = 52


def local(flow_state, match_elem, match_coord, match_dest, roughness):
    faces = [((128, 128), F32), ((128, 128), F32), ((8, 128), F32), ((8, 128), F32)]
    nodal = ((256, 8, 128), F32)
    flow_rows = flow_state.transpose(1, 0, 2).reshape(5, 8, 8, 8, 128).transpose(0, 1, 3, 2, 4).reshape(5, 512, 128)
    dest = match_dest.reshape(64, 128)
    elem = match_elem.reshape(1, M_DEV)
    rough = roughness.reshape(N_WALL * PER, 128)
    v, table, x1, x2, z1, z2 = call(
        entropy_kernel,
        [flow_rows],
        [nodal, ((1536, 256), BF16)] + faces,
        [((5, 512, 128), F32), pltpu.SemaphoreType.DMA((4,))],
        name="entropy",
        specs=[HBM],
        limit=ENTROPY_LIMIT,
    )
    rank, hot = call(
        rank_kernel,
        [match_dest.reshape(1, M_DEV)],
        [((64, 128), jnp.int32), ((256, M_DEV), BF16)],
        [((2048, 128), BF16), ((2048, 256), F32)],
        name="rank",
    )
    probes = []
    for i, (first, last) in enumerate(zip(CUTS[:-1], CUTS[1:])):
        (probe,) = call(
            lambda *refs, first=first, last=last: probe_kernel(first, last, *refs),
            [after(table, probes[-1]) if probes else after(table, rank), elem, match_coord],
            [((4, (last - first) * PROBE_BLOCK // 128, 128), F32)],
            name=f"probe{i}",
            cost=5,
        )
        probes.append(probe)
    halos = [*exchange("slab", x1, after(x2, rank), "vx")]
    halos += exchange("wall", after(z1, probes[0]), after(z2, probes[1]), "vz")
    part, f1, f2, zup, zlow = call(
        flux_kernel,
        [after(v, probes[-1]), *halos],
        [nodal] + faces,
        [((768, 8, 128), F32), ((768, 8, 128), F32)],
        name="flux",
        limit=12,
    )
    send, own = call(
        send_kernel,
        [*probes, after(rank, f1), dest, hot, rough, zup, zlow],
        [((N_WALL * CHUNK, 128), F32), ((3, 64, 128), F32)],
        [((576, M_DEV), BF16)],
        name="send",
        cost=3,
        limit=16,
    )
    got = lax.all_to_all(send.reshape(N_WALL, 1, CHUNK * 128), "wall", 0, 0, tiled=True)
    halos = exchange("slab", f1, after(f2, send), "fx")
    rate, wall = call(
        final_kernel,
        [part, *halos, got.reshape(N_WALL * CHUNK, 128), own, rank, dest, rough],
        [((2048, 128), F32), ((2 * N_WALL * PER, 128), F32)],
        [
            ((PER * N_WALL, 256), BF16),
            ((64, 128), F32),
            ((256, 128), F32),
            ((2048, 128), F32),
            pltpu.SemaphoreType.DMA((4,)),
        ],
        name="final",
        out_specs=[HBM, VMEM],
    )
    rate = rate.reshape(64, 8, 4, 128).transpose(0, 2, 1, 3).reshape(64, 4, 1024)
    wall_shear = wall.reshape(N_WALL * PER, 2, 128).transpose(1, 0, 2).reshape(2, N_WALL * CAP)
    return (rate, wall_shear)


def solution(mesh):
    return jax.shard_map(
        local,
        mesh=mesh,
        in_specs=(
            P(None, None, ("slab", "wall")),
            P(("slab", "wall")),
            P(None, ("slab", "wall")),
            P(("slab", "wall"), None),
            P(("slab", "wall")),
        ),
        out_specs=(P(None, None, ("slab", "wall")), P(None, ("slab", "wall"))),
        check_vma=False,
    )
```

time: 72.9 us -> 54.4 us (0.75)
  starting transfers between devices: 35.3 us -> 16 us
  waiting for transfers between devices: 3.26 us -> 13.4 us
  Pallas kernels: 27.2 us -> 22.3 us
  local copies, waits for them, and re-layouts: 5.28 us -> 0.77 us
    all_to_all x2 -> x1, starting transfers between devices: 21.1 us -> 4.91 us  [local(): lax.all_to_all(send.reshape(N_WALL, 1, CHUNK * 128), 'wall', 0, 0, tiled=...]
    all_to_all x2 -> x1, waiting for transfers between devices: 0.01 us -> 10.8 us  [local(): lax.all_to_all(send.reshape(N_WALL, 1, CHUNK * 128), 'wall', 0, 0, tiled=...]
    pallas_call x5 -> x8, Pallas kernels: 27.2 us -> 22.3 us  [call(): pl.pallas_call(kernel, out_shape=[jax.ShapeDtypeStruct(shape, dtype) for...]
    unnamed x13 -> x10, local copies, waits for them, and re-layouts: 4.4 us -> 0.77 us
    ppermute x8 -> x6, starting transfers between devices: 14.2 us -> 11.1 us  [the longest x3 7.42 us: exchange(): lax.ppermute(second, axis, [(i, (i - 1 + 2 * (i % 2)) % count) for i in r...]
    all_to_all x2 -> x0, local copies, waits for them, and re-layouts: 0.84 us -> none  [local(): lax.all_to_all(outgoing, 'wall', split_axis=1, concat_axis=1, tiled=True)]
    ppermute x8 -> x6, waiting for transfers between devices: 3.26 us -> 2.65 us  [the longest x3 2.64 us: exchange(): lax.ppermute(second, axis, [(i, (i - 1 + 2 * (i % 2)) % count) for i in r...]
  transfers between devices with their start and end apart: 10 -> 7, of which waited for: 2 -> 3; matrix products, arithmetic and copies ran while one was open for 0% -> 0% of each run, Pallas kernels for 23% -> 20%
where the time goes in v1:
time: 54.4 us; the launch traced here: 53.4 us
  Pallas kernels  22.3 us (41%)
  starting transfers between devices  16 us (29%)
  waiting for transfers between devices  13.4 us (25%)
  between operations  0.94 us (2%)
  local copies, waits for them, and re-layouts  0.77 us (1%)
    pallas_call x8, Pallas kernels, call(): pl.pallas_call(kernel, out_shape=[jax.ShapeDtypeStruct(shape, dtype) for...  22.3 us
    all_to_all x1, waiting for transfers between devices, local(): lax.all_to_all(send.reshape(N_WALL, 1, CHUNK * 128), 'wall', 0, 0, tiled=...  10.8 us
    ppermute x3, starting transfers between devices, exchange(): lax.ppermute(second, axis, [(i, (i - 1 + 2 * (i % 2)) % count) for i in r...  7.42 us
    all_to_all x1, starting transfers between devices, local(): lax.all_to_all(send.reshape(N_WALL, 1, CHUNK * 128), 'wall', 0, 0, tiled=...  4.91 us
    ppermute x3, starting transfers between devices, exchange(): lax.ppermute(first, axis, [(i, i + 1 - 2 * (i % 2)) for i in range(count)])  3.67 us
    ppermute x3, waiting for transfers between devices, exchange(): lax.ppermute(second, axis, [(i, (i - 1 + 2 * (i % 2)) % count) for i in r...  2.64 us
  transfers between devices with their start and end apart: 7, of which 3 were waited for; matrix products, arithmetic and copies ran while one was open for 0% of the time, Pallas kernels for 20%

profile of v1, /device:TPU:8, one launch (start us, length us, event | category | flops | bytes accessed | tf_op | source)
XLA Modules:
  0.0 53.4 jit_solution(3710375154632107671)
XLA Ops:
  0.6 1.6 %entropy.1 = (f32[256,8,128]{2,1,0:T(8,128)S(1)}, bf16[1536,256]{1,0:T(8,128)(2,1)S(1)}, f32[128,128]{1,0:T(8,128)S(1)}, f32[128,128]{1,0:T(8,128)S(1)}, f32[8,128]{1,0:T(8,128)S(1)}, /*index=5*/f32[8,128]{1,0:T(8,128)S(1)}) custom-call(f32[5,512,128]{2,1,0:T(8,128)} %bitcast.32), custom_call_target="tpu_custom_call" | custom-call | flops 1000000000 | bytes 3000000 | tf_op jit(solution)/shard_map/entropy/pallas_call | solution.py:509
  2.3 0.1 collective-permute-start
  2.4 0.0 copy-start.3
  2.4 0.7 %copy-done.3 = s32[8192,1]{0,1:T(1,128)S(1)} copy-done((s32[8192,1]{0,1:T(1,128)S(1)}, s32[8192,1]{0,1:T(1,128)}, u32[]{:S(2)}) %copy-start.3) | copy-done | bytes 32792
  3.1 2.6 %rank.1 = (s32[64,128]{1,0:T(8,128)S(1)}, bf16[256,8192]{1,0:T(8,128)(2,1)S(1)}) custom-call(s32[1,8192]{1,0:T(1,128)S(1)} %bitcast.29), custom_call_target="tpu_custom_call" | custom-call | flops 1000000000 | bytes 3000000 | tf_op jit(solution)/shard_map/rank/pallas_call | solution.py:509
  5.7 2.0 %probe0.1.refs_0_ = f32[4,16,128]{2,1,0:T(8,128)S(1)} custom-call(bf16[1536,256]{1,0:T(8,128)(2,1)S(1)} %get-tuple-element.33.refs_0_, s32[1,8192]{1,0:T(1,128)S(1)} %bitcast.26, s32[3,8192]{1,0:T(4,128)S(1)} %copy-done), custom_call_target="tpu_custom_call" | custom-call | flops 5000000000 | bytes 15000000 | tf_op jit(solution)/shard_map/probe0/pallas_call | solution.py:509
  7.8 2.0 %collective-permute-start.2 = (f32[8,128]{1,0:T(8,128)S(1)}, f32[8,128]{1,0:T(8,128)S(1)}, u32[]{:S(2)}, u32[]{:S(2)}) collective-permute-start(f32[8,128]{1,0:T(8,128)S(1)} %get-tuple-element.39), channel_id=1, source_target_pairs={{0,1},{1,0},{2,3},{3,2},{4,5},{5,4},{6,7},{7,6},{8,9},{9,8},{10,11... | collective-permute-start | bytes 12296 | tf_op jit(solution)/shard_map/vz_first/ppermute | solution.py:524
  9.8 3.0 %probe1.1.refs_1_ = f32[4,24,128]{2,1,0:T(8,128)S(1)} custom-call(bf16[1536,256]{1,0:T(8,128)(2,1)S(1)} %get-tuple-element.33.refs_0_, s32[1,8192]{1,0:T(1,128)S(1)} %bitcast.27, s32[3,8192]{1,0:T(4,128)S(1)} %copy-done), custom_call_target="tpu_custom_call" | custom-call | flops 5000000000 | bytes 15000000 | tf_op jit(solution)/shard_map/probe1/pallas_call | solution.py:509
  12.8 7.2 %collective-permute-start.3 = (f32[8,128]{1,0:T(8,128)S(1)}, f32[8,128]{1,0:T(8,128)S(1)}, u32[]{:S(2)}, u32[]{:S(2)}) collective-permute-start(f32[8,128]{1,0:T(8,128)S(1)} %get-tuple-element.41), channel_id=1, source_target_pairs={{0,31},{1,2},{2,1},{3,4},{4,3},{5,6},{6,5},{7,8},{8,7},{9,10},{10,... | collective-permute-start | bytes 12296 | tf_op jit(solution)/shard_map/vz_second/ppermute | solution.py:526
  20.0 0.0 collective-permute-start.1
  20.0 3.0 %probe2.1.refs_2_ = f32[4,24,128]{2,1,0:T(8,128)S(1)} custom-call(bf16[1536,256]{1,0:T(8,128)(2,1)S(1)} %get-tuple-element.33.refs_0_, s32[1,8192]{1,0:T(1,128)S(1)} %bitcast.28, s32[3,8192]{1,0:T(4,128)S(1)} %copy-done), custom_call_target="tpu_custom_call" | custom-call | flops 5000000000 | bytes 15000000 | tf_op jit(solution)/shard_map/probe2/pallas_call | solution.py:509
  23.0 0.0 collective-permute-done.2.z1_ref
  23.1 0.0 collective-permute-done.3.z2_ref
  23.1 0.0 collective-permute-done.x1_ref
  23.1 0.6 %collective-permute-done.1.x2_ref = f32[128,128]{1,0:T(8,128)S(1)} collective-permute-done((f32[128,128]{1,0:T(8,128)S(1)}, f32[128,128]{1,0:T(8,128)S(1)}, u32[]{:S(2)}, u32[]{:S(2)}) %collective-permute-start.1) | collective-permute-done | bytes 65568 | tf_op jit(solution)/shard_map/vx_second/ppermute | solution.py:526
  23.7 2.5 %flux.1 = (f32[256,8,128]{2,1,0:T(8,128)S(1)}, f32[128,128]{1,0:T(8,128)S(1)}, f32[128,128]{1,0:T(8,128)S(1)}, f32[8,128]{1,0:T(8,128)S(1)}, f32[8,128]{1,0:T(8,128)S(1)}) custom-call(f32[256,8,128]{2,1,0:T(8,128)S(1)} %get-tuple-element.34.v_ref, f32[128,128]{1,0:T(8,128)S(1)} %collective-permute-done.x1_ref, f32[128,128]{1,0:T(8,128)S(1)} %collective-permute-done.1.x2_ref, ...), custom_call_target="tpu_custom_call" | custom-call | flops 1000000000 | bytes 3000000 | tf_op jit(solution)/shard_map/flux/pallas_call | solution.py:509
  26.2 3.8 %send.1 = (f32[768,128]{1,0:T(8,128)}, f32[3,64,128]{2,1,0:T(8,128)S(1)}) custom-call(f32[4,16,128]{2,1,0:T(8,128)S(1)} %probe0.1.refs_0_, f32[4,24,128]{2,1,0:T(8,128)S(1)} %probe1.1.refs_1_, f32[4,24,128]{2,1,0:T(8,128)S(1)} %probe2.1.refs_2_, s32[64,128]{1,0:T(8,128)S(1)} %get-tuple-element.45.refs_3_.rank_ref, s32[64,128]{1,0:T(8,128)S(1)} %bitcast.30, ...), custom_call_target="tpu_custom_call" | custom-call | flops 3000000000 | bytes 9000000 | tf_op jit(solution)/shard_map/send/pallas_call | solution.py:509
  30.0 4.9 %all-to-all-start = ((f32[32,1,3072]{2,1,0:T(1,128)}), f32[32,1,3072]{2,1,0:T(1,128)S(1)}, u32[]{:S(2)}, u32[]{:S(2)}) async-start(f32[32,1,3072]{2,1,0:T(1,128)} %bitcast.8), calls=%async_computation | async-start | bytes 786432 | tf_op jit(solution)/shard_map/all_to_all | solution.py:590
  34.9 0.2 collective-permute-start.5
  35.1 1.6 %collective-permute-start.4 = (f32[128,128]{1,0:T(8,128)S(1)}, f32[128,128]{1,0:T(8,128)S(1)}, u32[]{:S(2)}, u32[]{:S(2)}) collective-permute-start(f32[128,128]{1,0:T(8,128)S(1)} %get-tuple-element.43), channel_id=1, source_target_pairs={{0,32},{32,0},{64,96},{96,64},{128,160},{160,128},{192,224},{224,1... | collective-permute-start | bytes 196616 | tf_op jit(solution)/shard_map/fx_first/ppermute | solution.py:524
  36.7 2.0 %collective-permute-done.5.x2_ref = f32[128,128]{1,0:T(8,128)S(1)} collective-permute-done((f32[128,128]{1,0:T(8,128)S(1)}, f32[128,128]{1,0:T(8,128)S(1)}, u32[]{:S(2)}, u32[]{:S(2)}) %collective-permute-start.5) | collective-permute-done | bytes 65568 | tf_op jit(solution)/shard_map/fx_second/ppermute | solution.py:526
  38.7 0.0 collective-permute-done.4.x1_ref
  38.7 10.8 %all-to-all-done = f32[32,1,3072]{2,1,0:T(1,128)S(1)} async-done(((f32[32,1,3072]{2,1,0:T(1,128)}), f32[32,1,3072]{2,1,0:T(1,128)S(1)}, u32[]{:S(2)}, u32[]{:S(2)}) %all-to-all-start) | async-done | bytes 393248 | tf_op jit(solution)/shard_map/all_to_all | solution.py:590
  49.5 3.8 %final.1 = (f32[2048,128]{1,0:T(8,128)}, f32[320,128]{1,0:T(8,128)}) custom-call(f32[256,8,128]{2,1,0:T(8,128)S(1)} %get-tuple-element.42.part_ref, f32[128,128]{1,0:T(8,128)S(1)} %collective-permute-done.4.x1_ref, f32[128,128]{1,0:T(8,128)S(1)} %collective-permute-done.5.x2_ref, f32[768,128]{1,0:T(8,128)S(1)} %bitcast.23, ...), custom_call_target="tpu_custom_call" | custom-call | flops 1000000000 | bytes 3000000 | tf_op jit(solution)/shard_map/final/pallas_call | solution.py:509
  (8 shorter events, 0.0 us)
Async XLA Ops:
  0.6 5.1 %copy-start = (s32[3,8192]{1,0:T(4,128)S(1)}, s32[3,8192]{1,0:T(4,128)}, u32[]{:S(2)}) copy-start(s32[3,8192]{1,0:T(4,128)} %refs_2_.5) | copy-start | bytes 294916
  0.6 5.1 %copy-start.2 = (s32[8192]{0:T(1024)S(1)}, s32[8192]{0:T(1024)}, u32[]{:S(2)}) copy-start(s32[8192]{0:T(1024)} %param.6) | copy-start | bytes 98308
  2.3 20.8 %collective-permute-start = (f32[128,128]{1,0:T(8,128)S(1)}, f32[128,128]{1,0:T(8,128)S(1)}, u32[]{:S(2)}, u32[]{:S(2)}) collective-permute-start(f32[128,128]{1,0:T(8,128)S(1)} %get-tuple-element.35), channel_id=1, source_target_pairs={{0,32},{32,0},{64,96},{96,64},{128,160},{160,128},{192,224},{224,1... | collective-permute-start | bytes 196616 | tf_op jit(solution)/shard_map/vx_first/ppermute | solution.py:524
  2.4 0.8 %copy-start.3 = (s32[8192,1]{0,1:T(1,128)S(1)}, s32[8192,1]{0,1:T(1,128)}, u32[]{:S(2)}) copy-start(s32[8192,1]{0,1:T(1,128)} %param.8) | copy-start | bytes 98308
  7.8 15.3 %collective-permute-start.2 = (f32[8,128]{1,0:T(8,128)S(1)}, f32[8,128]{1,0:T(8,128)S(1)}, u32[]{:S(2)}, u32[]{:S(2)}) collective-permute-start(f32[8,128]{1,0:T(8,128)S(1)} %get-tuple-element.39), channel_id=1, source_target_pairs={{0,1},{1,0},{2,3},{3,2},{4,5},{5,4},{6,7},{7,6},{8,9},{9,8},{10,11... | collective-permute-start | bytes 12296 | tf_op jit(solution)/shard_map/vz_first/ppermute | solution.py:524
  12.8 10.3 %collective-permute-start.3 = (f32[8,128]{1,0:T(8,128)S(1)}, f32[8,128]{1,0:T(8,128)S(1)}, u32[]{:S(2)}, u32[]{:S(2)}) collective-permute-start(f32[8,128]{1,0:T(8,128)S(1)} %get-tuple-element.41), channel_id=1, source_target_pairs={{0,31},{1,2},{2,1},{3,4},{4,3},{5,6},{6,5},{7,8},{8,7},{9,10},{10,... | collective-permute-start | bytes 12296 | tf_op jit(solution)/shard_map/vz_second/ppermute | solution.py:526
  20.0 6.2 %copy-start.1 = (f32[20480]{0:T(1024)S(1)}, f32[20480]{0:T(1024)}, u32[]{:S(2)}) copy-start(f32[20480]{0:T(1024)} %param.9) | copy-start | bytes 245764
  20.0 6.2 %copy-start.4 = (s32[8192,1]{0,1:T(1,128)S(1)}, s32[8192,1]{0,1:T(1,128)}, u32[]{:S(2)}) copy-start(s32[8192,1]{0,1:T(1,128)} %param.8) | copy-start | bytes 98308
  20.0 3.7 %collective-permute-start.1 = (f32[128,128]{1,0:T(8,128)S(1)}, f32[128,128]{1,0:T(8,128)S(1)}, u32[]{:S(2)}, u32[]{:S(2)}) collective-permute-start(f32[128,128]{1,0:T(8,128)S(1)} %get-tuple-element.37), channel_id=1, source_target_pairs={{0,224},{32,64},{64,32},{96,128},{128,96},{160,192},{192,160},{224... | collective-permute-start | bytes 196616 | tf_op jit(solution)/shard_map/vx_second/ppermute | solution.py:526
  30.0 19.5 %all-to-all-start = ((f32[32,1,3072]{2,1,0:T(1,128)}), f32[32,1,3072]{2,1,0:T(1,128)S(1)}, u32[]{:S(2)}, u32[]{:S(2)}) async-start(f32[32,1,3072]{2,1,0:T(1,128)} %bitcast.8), calls=%async_computation | async-start | bytes 786432 | tf_op jit(solution)/shard_map/all_to_all | solution.py:590
  34.9 3.8 %collective-permute-start.5 = (f32[128,128]{1,0:T(8,128)S(1)}, f32[128,128]{1,0:T(8,128)S(1)}, u32[]{:S(2)}, u32[]{:S(2)}) collective-permute-start(f32[128,128]{1,0:T(8,128)S(1)} %get-tuple-element.50), channel_id=1, source_target_pairs={{0,224},{32,64},{64,32},{96,128},{128,96},{160,192},{192,160},{224... | collective-permute-start | bytes 196616 | tf_op jit(solution)/shard_map/fx_second/ppermute | solution.py:526
  35.1 3.6 %collective-permute-start.4 = (f32[128,128]{1,0:T(8,128)S(1)}, f32[128,128]{1,0:T(8,128)S(1)}, u32[]{:S(2)}, u32[]{:S(2)}) collective-permute-start(f32[128,128]{1,0:T(8,128)S(1)} %get-tuple-element.43), channel_id=1, source_target_pairs={{0,32},{32,0},{64,96},{96,64},{128,160},{160,128},{192,224},{224,1... | collective-permute-start | bytes 196616 | tf_op jit(solution)/shard_map/fx_first/ppermute | solution.py:524

commit v2 on v1

--- a/solution.py
+++ b/solution.py
@@ -121,6 +121,17 @@
     first = first_ref[pl.ds(8 * block, 8), :]
     second = second_ref[pl.ds(8 * block, 8), :]
     return pick(even, second, first), pick(even, first, second)
+
+
+def join_x(u, halos, i, row):
+    prev_halo, next_halo = halos
+    if i:
+        prev_halo = pltpu.roll(prev_halo, 8 - 2 * i, 0)
+    if i != 3:
+        next_halo = pltpu.roll(next_halo, 6 - 2 * i, 0)
+    prev = jnp.where(row < 2, prev_halo, pltpu.roll(u[3], 2, 0))
+    following = jnp.where(row >= 6, next_halo, pltpu.roll(u[0], 6, 0))
+    return prev, following
 
 
 def entropy_kernel(flow_ref, v_ref, table_ref, x1_ref, x2_ref, z1_ref, z2_ref, rows_ref, sems):
@@ -168,8 +179,11 @@
     return prev, following
 
 
+FLUX = ((0, 1, 2, 6), (1, 3, 4, 7), (2, 4, 5, 8))
+
+
 def flux_kernel(v_ref, x1_ref, x2_ref, z1_ref, z2_ref,
-                rate_ref, f1_ref, f2_ref, zup_ref, zlow_ref, g_ref, f_ref):
+                rate_ref, fx1_ref, fx2_ref, fz1_ref, fz2_ref, g_ref, f_ref):
     row = iota((8, 128), 0)
     lane = iota((8, 128), 1)
     odd = row % 2 == 1
@@ -184,14 +198,7 @@
             u = [v_ref[comp * 64 + n] for n in nodes]
             d = list(line_derivative(*u))
             if direction == 0:
-                i = k % 4
-                prev_halo, next_halo = x_halos(x1_ref, x2_ref, k // 4)
-                if i:
-                    prev_halo = pltpu.roll(prev_halo, 8 - 2 * i, 0)
-                if i != 3:
-                    next_halo = pltpu.roll(next_halo, 6 - 2 * i, 0)
-                prev = jnp.where(row < 2, prev_halo, pltpu.roll(u[3], 2, 0))
-                following = jnp.where(row >= 6, next_halo, pltpu.roll(u[0], 6, 0))
+                prev, following = join_x(u, x_halos(x1_ref, x2_ref, k // 4), k % 4, row)
             elif direction == 1:
                 prev, following = jumps_y(u[0], u[3])
             else:
@@ -223,25 +230,26 @@
                 tau[i][d] = entry
         for d in range(3):
             heat = u[0] * tau[d][0] + u[1] * tau[d][1] + u[2] * tau[d][2] + conduct * g[d][3]
-            for c in range(3):
-                f_ref[(d * 4 + c) * 64 + n] = tau[d][c]
-            f_ref[(d * 4 + 3) * 64 + n] = heat
+            for c in range(d, 3):
+                f_ref[FLUX[d][c] * 64 + n] = tau[d][c]
+            f_ref[FLUX[d][3] * 64 + n] = heat
         return carry
 
     lax.fori_loop(0, 64, pointwise, 0, unroll=4)
 
     def face(direction, end):
-        return lambda k: f_ref[(direction * 4 + k // 16) * 64 + line_nodes(direction, k % 16)[end]]
-
-    pack_x(face(0, 0), face(0, 3), f1_ref, f2_ref)
-    zup_ref[...], zlow_ref[...] = pack_z(face(2, 0), face(2, 3))
-
+        return lambda k: f_ref[FLUX[direction][k // 16] * 64 + line_nodes(direction, k % 16)[end]]
+
+    pack_x(face(0, 0), face(0, 3), fx1_ref, fx2_ref)
+    upper, lower = pack_z(face(2, 0), face(2, 3))
+    fz1_ref[...] = pick(even, upper, lower)
+    fz2_ref[...] = pick(even, lower, upper)
 
     for comp in range(4):
         for direction in range(3):
             for line in range(16):
                 nodes = line_nodes(direction, line)
-                u = [f_ref[(direction * 4 + comp) * 64 + n] for n in nodes]
+                u = [f_ref[FLUX[direction][comp] * 64 + n] for n in nodes]
                 d = list(line_derivative(*u))
                 if direction == 0:
                     prev = jnp.where(row < 2, 0.0, pltpu.roll(u[3], 2, 0))
@@ -263,11 +271,56 @@
                         rate_ref[where] = rate_ref[where] + d[end]
 
 
+def assemble_kernel(part_ref, x1_ref, x2_ref, z1_ref, z2_ref, rate_ref, bottom_ref, out_ref, sems):
+    row = iota((8, 128), 0)
+    lane = iota((8, 128), 1)
+    even = is_even("wall")
+    z_prev = pick(even, z2_ref[...], z1_ref[...])
+    z_next = pick(even, z1_ref[...], z2_ref[...])
+    copies = []
+    for n in range(64):
+        a, b, c = n // 16, n // 4 % 4, n % 4
+        for comp in range(4):
+            total = part_ref[comp * 64 + n]
+            if a in (0, 3):
+                k = comp * 16 + 4 * b + c
+                i = k % 4
+                halo = x_halos(x1_ref, x2_ref, k // 4)[0 if a == 0 else 1]
+                shift = (8 - 2 * i) % 8 if a == 0 else 6 - 2 * i
+                if shift:
+                    halo = pltpu.roll(halo, shift, 0)
+                if a == 0:
+                    total = total - jnp.where(row < 2, 3.0 * halo, 0.0)
+                else:
+                    total = total + jnp.where(row >= 6, 3.0 * halo, 0.0)
+            if c in (0, 3):
+                k = comp * 16 + 4 * a + b
+                halo = z_prev if c == 0 else z_next
+                shift = (128 - k) % 128 if c == 0 else 127 - k
+                if shift:
+                    halo = pltpu.roll(halo, shift, 1)
+                if c == 0:
+                    total = total - jnp.where(lane == 0, 3.0 * halo, 0.0)
+                else:
+                    total = total + jnp.where(lane == 127, 3.0 * halo, 0.0)
+            if b == 0:
+                bottom_ref[(4 * a + c) * 4 + comp] = total
+            else:
+                out_ref[pl.ds(n * 32 + comp, 8, stride=4), :] = total
+        if n % 16 == 15:
+            span = pl.ds(512 * a + 128, 384)
+            copies.append(pltpu.make_async_copy(out_ref.at[span], rate_ref.at[span], sems.at[a]))
+            copies[-1].start()
+    for copy in copies:
+        copy.wait()
+
+
 def rank_kernel(dest_ref, rank_ref, hot_ref, named_ref, count_ref):
     before = (iota((128, 128), 0) < iota((128, 128), 1)).astype(F32).astype(BF16)
     counter = jnp.concatenate([before, jnp.ones((128, 128), BF16)], axis=1)
     wall_ids = iota((N_WALL, 128), 0)
-    low_ids = iota((256, 128), 0)
+    low_ids = iota((256, 128), 0).astype(jnp.int16)
+    one, zero = jnp.ones((), BF16), jnp.zeros((), BF16)
     blocks = M_DEV // 128
     for block in range(blocks):
         named = (wall_ids == dest_ref[0:1, 128 * block : 128 * block + 128]).astype(F32).astype(BF16)
@@ -280,7 +333,8 @@
         own = wall_ids == dest_ref[0:1, 128 * block : 128 * block + 128]
         rank = jnp.sum(jnp.where(own, count_ref[rows, :128] + total, 0.0), axis=0, keepdims=True).astype(jnp.int32)
         rank_ref[pl.ds(block, 1), :] = rank
-        hot_ref[:, lanes] = (low_ids == (rank & 255)).astype(F32).astype(BF16)
+        low = jnp.broadcast_to(rank & 255, (256, 128)).astype(jnp.int16)
+        hot_ref[:, lanes] = jnp.where(low_ids == low, one, zero)
         total = total + count_ref[rows, 128:]
 
 
@@ -345,13 +399,13 @@
 
 SEND_BLOCK = 1024
 PER = CAP // 128
-CHUNK = 4 * PER + 4
+CHUNK = 4 * PER
 
 
 def send_kernel(*refs):
-    n_probe = len(refs) - 9
+    n_probe = len(refs) - 7
     probe_refs = refs[:n_probe]
-    rank_ref, dest_ref, hot_ref, rough_ref, zup_ref, zlow_ref, send_ref, own_ref, lhs_ref = refs[n_probe:]
+    rank_ref, dest_ref, hot_ref, rough_ref, send_ref, own_ref, lhs_ref = refs[n_probe:]
     rows = M_DEV // 128
     rho, mx, mz, height = [jnp.concatenate([ref[f] for ref in probe_refs], axis=0) for f in range(4)]
     inv_rho = 1.0 / rho
@@ -395,15 +449,6 @@
             ]
 
 
-    half = iota((4, 128), 1) < 64
-    upper, lower = [
-        jnp.where(half, ref[0:4, :], pltpu.roll(ref[...], 64, 1)[4:8]) for ref in (zup_ref, zlow_ref)
-    ]
-    target = lax.rem(lax.axis_index("wall") + 1, N_WALL)
-    for w in range(N_WALL):
-        send_ref[pl.ds(w * CHUNK + 4 * PER, 4), :] = jnp.where(target == w, upper, lower)
-
-
 def shear_scale(log_term):
     ratio = jnp.ones_like(log_term)
     for sweep in range(NEWTON):
@@ -412,18 +457,8 @@
     return 1.0 / (ratio * ratio)
 
 
-def final_kernel(part_ref, x1_ref, x2_ref, got_ref, own_ref, rank_ref, dest_ref, rough_ref,
+def final_kernel(kept_ref, bottom_ref, got_ref, own_ref, rank_ref, dest_ref, rough_ref,
                  rate_ref, wall_ref, table_ref, factor_ref, shear_ref, out_ref, sems):
-    row = iota((8, 128), 0)
-    lane = iota((8, 128), 1)
-    here = lax.axis_index("wall")
-    z_halo = []
-    for source in (here + N_WALL - 1, here + 1):
-        start = pl.multiple_of(lax.rem(source, N_WALL) * CHUNK + 4 * PER - 4, 8)
-        folded = got_ref[pl.ds(start, 8), :]
-        unfolded = pltpu.roll(folded, 64, 1)
-        z_halo.append(jnp.concatenate([folded[4:8], unfolded[4:8]], axis=0))
-
     for chunk in range(PER):
         for w in range(0, N_WALL, 16):
             value = jnp.concatenate(
@@ -433,13 +468,12 @@
             table_ref[pl.ds(chunk * N_WALL + w, 16), :128] = high
             table_ref[pl.ds(chunk * N_WALL + w, 16), 128:] = (value - high.astype(F32)).astype(BF16)
     code = (rank_ref[...] >> 7) * N_WALL + dest_ref[...]
-    place = rank_ref[...] & 127
     code_ids = iota((PER * N_WALL, 128), 0)
-    ids = iota((128, 128), 0)
+    ids = iota((128, 512), 0).astype(jnp.int16)
+    one, zero = jnp.ones((), BF16), jnp.zeros((), BF16)
     for block in range(M_DEV // 512):
-        hot = jnp.concatenate(
-            [jnp.where(ids == place[r : r + 1], 1.0, 0.0).astype(BF16) for r in range(4 * block, 4 * block + 4)], axis=1
-        )
+        place = jnp.concatenate([rank_ref[r : r + 1, :] & 127 for r in range(4 * block, 4 * block + 4)], axis=1)
+        hot = jnp.where(ids == jnp.broadcast_to(place, (128, 512)).astype(jnp.int16), one, zero)
         found = jnp.dot(table_ref[...], jnp.concatenate([hot, hot], axis=0), preferred_element_type=F32)
         for i in range(4):
             r = 4 * block + i
@@ -451,6 +485,18 @@
         shear = own_ref[comp] * scale
         for pair in range(16):
             shear_ref[pl.ds(128 * comp + 8 * pair, 4, stride=2), :] = shear[4 * pair : 4 * pair + 4]
+    copies = []
+    for a in range(4):
+        for c in range(4):
+            for comp in range(4):
+                total = bottom_ref[(4 * a + c) * 4 + comp]
+                if comp in (0, 2):
+                    total = total - 6.0 * shear_ref[pl.ds((comp // 2) * 128 + (4 * a + c) * 8, 8), :]
+                out_ref[pl.ds(128 * a + 32 * c + comp, 8, stride=4), :] = total
+        copies.append(
+            pltpu.make_async_copy(out_ref.at[pl.ds(128 * a, 128)], rate_ref.at[pl.ds(512 * a, 128)], sems.at[a])
+        )
+        copies[-1].start()
 
     for chunk in range(PER):
         for w in range(0, N_WALL, 8):
@@ -464,39 +510,6 @@
             wall_ref[pl.ds(place, 8, stride=2 * PER), :] = jnp.where(used, vx * scale, 0.0)
             wall_ref[pl.ds(place + 1, 8, stride=2 * PER), :] = jnp.where(used, vz * scale, 0.0)
 
-    copies = []
-    for n in range(64):
-        a, b, c = n // 16, n // 4 % 4, n % 4
-        for comp in range(4):
-            total = part_ref[comp * 64 + n]
-            if a in (0, 3):
-                k = comp * 16 + 4 * b + c
-                i = k % 4
-                halo = x_halos(x1_ref, x2_ref, k // 4)[0 if a == 0 else 1]
-                shift = (8 - 2 * i) % 8 if a == 0 else 6 - 2 * i
-                if shift:
-                    halo = pltpu.roll(halo, shift, 0)
-                if a == 0:
-                    total = total - jnp.where(row < 2, 3.0 * halo, 0.0)
-                else:
-                    total = total + jnp.where(row >= 6, 3.0 * halo, 0.0)
-            if c in (0, 3):
-                k = comp * 16 + 4 * a + b
-                halo = z_halo[0 if c == 0 else 1]
-                shift = (128 - k) % 128 if c == 0 else 127 - k
-                if shift:
-                    halo = pltpu.roll(halo, shift, 1)
-                if c == 0:
-                    total = total - jnp.where(lane == 0, 3.0 * halo, 0.0)
-                else:
-                    total = total + jnp.where(lane == 127, 3.0 * halo, 0.0)
-            if b == 0 and comp in (0, 2):
-                total = total - 6.0 * shear_ref[pl.ds((comp // 2) * 128 + (4 * a + c) * 8, 8), :]
-            out_ref[pl.ds(n * 32 + comp, 8, stride=4), :] = total
-        if n % 16 == 15:
-            span = pl.ds(512 * a, 512)
-            copies.append(pltpu.make_async_copy(out_ref.at[span], rate_ref.at[span], sems.at[a]))
-            copies[-1].start()
     for copy in copies:
         copy.wait()
 
@@ -505,7 +518,7 @@
 HBM = pl.BlockSpec(memory_space=pltpu.HBM)
 
 
-def call(kernel, inputs, outputs, scratch=(), name=None, cost=1, specs=None, out_specs=None, limit=8):
+def call(kernel, inputs, outputs, scratch=(), name=None, cost=1, specs=None, out_specs=None, limit=8, aliases={}):
     return pl.pallas_call(
         kernel,
         out_shape=[jax.ShapeDtypeStruct(shape, dtype) for shape, dtype in outputs],
@@ -513,6 +526,7 @@
         out_specs=out_specs or [VMEM] * len(outputs),
         scratch_shapes=[s if not isinstance(s, tuple) else pltpu.VMEM(*s) for s in scratch],
         name=name,
+        input_output_aliases=aliases,
         cost_estimate=pl.CostEstimate(flops=cost * 10**9, bytes_accessed=cost * 3 * 10**6, transcendentals=0),
         compiler_params=pltpu.CompilerParams(vmem_limit_bytes=int(limit * 1024 * 1024)),
     )(*inputs)
@@ -570,17 +584,9 @@
         probes.append(probe)
     halos = [*exchange("slab", x1, after(x2, rank), "vx")]
     halos += exchange("wall", after(z1, probes[0]), after(z2, probes[1]), "vz")
-    part, f1, f2, zup, zlow = call(
-        flux_kernel,
-        [after(v, probes[-1]), *halos],
-        [nodal] + faces,
-        [((768, 8, 128), F32), ((768, 8, 128), F32)],
-        name="flux",
-        limit=12,
-    )
     send, own = call(
         send_kernel,
-        [*probes, after(rank, f1), dest, hot, rough, zup, zlow],
+        [*probes, after(rank, *halos), dest, hot, rough],
         [((N_WALL * CHUNK, 128), F32), ((3, 64, 128), F32)],
         [((576, M_DEV), BF16)],
         name="send",
@@ -588,20 +594,38 @@
         limit=16,
     )
     got = lax.all_to_all(send.reshape(N_WALL, 1, CHUNK * 128), "wall", 0, 0, tiled=True)
-    halos = exchange("slab", f1, after(f2, send), "fx")
+    part, x1, x2, z1, z2 = call(
+        flux_kernel,
+        [after(v, send), *halos],
+        [nodal] + faces,
+        [((768, 8, 128), F32), ((576, 8, 128), F32)],
+        name="flux",
+        limit=12,
+    )
+    halos = [*exchange("slab", x1, x2, "fx"), *exchange("wall", z1, z2, "fz")]
+    rate, bottom = call(
+        assemble_kernel,
+        [part, *halos],
+        [((2048, 128), F32), ((64, 8, 128), F32)],
+        [((2048, 128), F32), pltpu.SemaphoreType.DMA((4,))],
+        name="assemble",
+        out_specs=[HBM, VMEM],
+    )
     rate, wall = call(
         final_kernel,
-        [part, *halos, got.reshape(N_WALL * CHUNK, 128), own, rank, dest, rough],
+        [rate, bottom, got.reshape(N_WALL * CHUNK, 128), own, rank, dest, rough],
         [((2048, 128), F32), ((2 * N_WALL * PER, 128), F32)],
         [
             ((PER * N_WALL, 256), BF16),
             ((64, 128), F32),
             ((256, 128), F32),
-            ((2048, 128), F32),
+            ((512, 128), F32),
             pltpu.SemaphoreType.DMA((4,)),
         ],
         name="final",
+        specs=[HBM] + [VMEM] * 6,
         out_specs=[HBM, VMEM],
+        aliases={0: 0},
     )
     rate = rate.reshape(64, 8, 4, 128).transpose(0, 2, 1, 3).reshape(64, 4, 1024)
     wall_shear = wall.reshape(N_WALL * PER, 2, 128).transpose(1, 0, 2).reshape(2, N_WALL * CAP)

time: 54.4 us -> 49.2 us (0.904); the launches traced: 53.4 us -> 48.9 us
  waiting for transfers between devices: 13.4 us -> 3.24 us
  starting transfers between devices: 16 us -> 22.6 us
  Pallas kernels: 22.3 us -> 21.3 us
    all_to_all x1, waiting for transfers between devices: 10.8 us -> 0.01 us  [local(): lax.all_to_all(send.reshape(N_WALL, 1, CHUNK * 128), 'wall', 0, 0, tiled=...]
    ppermute x3 -> x4, starting transfers between devices: 7.42 us -> 13.6 us  [exchange(): lax.ppermute(second, axis, [(i, (i - 1 + 2 * (i % 2)) % count) for i in r...]
    pallas_call x8 -> x9, Pallas kernels: 22.3 us -> 21.3 us  [call(): pl.pallas_call(kernel, out_shape=[jax.ShapeDtypeStruct(shape, dtype) for...]
    ppermute x3 -> x4, waiting for transfers between devices: 2.64 us -> 3.22 us  [exchange(): lax.ppermute(second, axis, [(i, (i - 1 + 2 * (i % 2)) % count) for i in r...]
    ppermute x3 -> x4, starting transfers between devices: 3.67 us -> 4.17 us  [exchange(): lax.ppermute(first, axis, [(i, i + 1 - 2 * (i % 2)) for i in range(count)])]
  transfers between devices with their start and end apart: 7 -> 9, of which waited for: 3 -> 2; matrix products, arithmetic and copies ran while one was open for 0% -> 0% of each run, Pallas kernels for 20% -> 27%
where the time goes in v2:
time: 49.2 us; the launch traced here: 48.9 us
  starting transfers between devices  22.6 us (46%)
  Pallas kernels  21.3 us (43%)
  waiting for transfers between devices  3.24 us (7%)
  between operations  0.94 us (2%)
  local copies, waits for them, and re-layouts  0.77 us (2%)
    pallas_call x9, Pallas kernels, call(): pl.pallas_call(kernel, out_shape=[jax.ShapeDtypeStruct(shape, dtype) for...  21.3 us
    ppermute x4, starting transfers between devices, exchange(): lax.ppermute(second, axis, [(i, (i - 1 + 2 * (i % 2)) % count) for i in r...  13.6 us
    all_to_all x1, starting transfers between devices, local(): lax.all_to_all(send.reshape(N_WALL, 1, CHUNK * 128), 'wall', 0, 0, tiled=...  4.92 us
    ppermute x4, starting transfers between devices, exchange(): lax.ppermute(first, axis, [(i, i + 1 - 2 * (i % 2)) for i in range(count)])  4.17 us
    ppermute x4, waiting for transfers between devices, exchange(): lax.ppermute(second, axis, [(i, (i - 1 + 2 * (i % 2)) % count) for i in r...  3.22 us
  transfers between devices with their start and end apart: 9, of which 2 were waited for; matrix products, arithmetic and copies ran while one was open for 0% of the time, Pallas kernels for 27%

profile of v2, /device:TPU:8, one launch (start us, length us, event | category | flops | bytes accessed | tf_op | source)
XLA Modules:
  0.0 48.9 jit_solution(15587365850883281619)
XLA Ops:
  0.6 1.6 %entropy.1 = (f32[256,8,128]{2,1,0:T(8,128)S(1)}, bf16[1536,256]{1,0:T(8,128)(2,1)S(1)}, f32[128,128]{1,0:T(8,128)S(1)}, f32[128,128]{1,0:T(8,128)S(1)}, f32[8,128]{1,0:T(8,128)S(1)}, /*index=5*/f32[8,128]{1,0:T(8,128)S(1)}) custom-call(f32[5,512,128]{2,1,0:T(8,128)} %bitcast.32), custom_call_target="tpu_custom_call" | custom-call | flops 1000000000 | bytes 3000000 | tf_op jit(solution)/shard_map/entropy/pallas_call | solution.py:522
  2.3 0.1 collective-permute-start
  2.4 0.0 copy-start.3
  2.4 0.7 %copy-done.3 = s32[8192,1]{0,1:T(1,128)S(1)} copy-done((s32[8192,1]{0,1:T(1,128)S(1)}, s32[8192,1]{0,1:T(1,128)}, u32[]{:S(2)}) %copy-start.3) | copy-done | bytes 32792
  3.1 1.6 %rank.1 = (s32[64,128]{1,0:T(8,128)S(1)}, bf16[256,8192]{1,0:T(8,128)(2,1)S(1)}) custom-call(s32[1,8192]{1,0:T(1,128)S(1)} %bitcast.29), custom_call_target="tpu_custom_call" | custom-call | flops 1000000000 | bytes 3000000 | tf_op jit(solution)/shard_map/rank/pallas_call | solution.py:522
  4.8 2.0 %probe0.1.refs_0_ = f32[4,16,128]{2,1,0:T(8,128)S(1)} custom-call(bf16[1536,256]{1,0:T(8,128)(2,1)S(1)} %get-tuple-element.34.refs_0_, s32[1,8192]{1,0:T(1,128)S(1)} %bitcast.26, s32[3,8192]{1,0:T(4,128)S(1)} %copy-done), custom_call_target="tpu_custom_call" | custom-call | flops 5000000000 | bytes 15000000 | tf_op jit(solution)/shard_map/probe0/pallas_call | solution.py:522
  6.8 2.0 %collective-permute-start.2 = (f32[8,128]{1,0:T(8,128)S(1)}, f32[8,128]{1,0:T(8,128)S(1)}, u32[]{:S(2)}, u32[]{:S(2)}) collective-permute-start(f32[8,128]{1,0:T(8,128)S(1)} %get-tuple-element.39), channel_id=1, source_target_pairs={{0,1},{1,0},{2,3},{3,2},{4,5},{5,4},{6,7},{7,6},{8,9},{9,8},{10,11... | collective-permute-start | bytes 12296 | tf_op jit(solution)/shard_map/vz_first/ppermute | solution.py:538
  8.8 3.0 %probe1.1.refs_1_ = f32[4,24,128]{2,1,0:T(8,128)S(1)} custom-call(bf16[1536,256]{1,0:T(8,128)(2,1)S(1)} %get-tuple-element.34.refs_0_, s32[1,8192]{1,0:T(1,128)S(1)} %bitcast.27, s32[3,8192]{1,0:T(4,128)S(1)} %copy-done), custom_call_target="tpu_custom_call" | custom-call | flops 5000000000 | bytes 15000000 | tf_op jit(solution)/shard_map/probe1/pallas_call | solution.py:522
  11.8 7.2 %collective-permute-start.3 = (f32[8,128]{1,0:T(8,128)S(1)}, f32[8,128]{1,0:T(8,128)S(1)}, u32[]{:S(2)}, u32[]{:S(2)}) collective-permute-start(f32[8,128]{1,0:T(8,128)S(1)} %get-tuple-element.41), channel_id=1, source_target_pairs={{0,31},{1,2},{2,1},{3,4},{4,3},{5,6},{6,5},{7,8},{8,7},{9,10},{10,... | collective-permute-start | bytes 12296 | tf_op jit(solution)/shard_map/vz_second/ppermute | solution.py:540
  19.1 3.0 %probe2.1.refs_2_ = f32[4,24,128]{2,1,0:T(8,128)S(1)} custom-call(bf16[1536,256]{1,0:T(8,128)(2,1)S(1)} %get-tuple-element.34.refs_0_, s32[1,8192]{1,0:T(1,128)S(1)} %bitcast.28, s32[3,8192]{1,0:T(4,128)S(1)} %copy-done), custom_call_target="tpu_custom_call" | custom-call | flops 5000000000 | bytes 15000000 | tf_op jit(solution)/shard_map/probe2/pallas_call | solution.py:522
  22.1 0.0 collective-permute-done.2.z1_ref
  22.1 0.0 collective-permute-done.3.z2_ref
  22.1 0.6 %collective-permute-done.1.x2_ref = f32[128,128]{1,0:T(8,128)S(1)} collective-permute-done((f32[128,128]{1,0:T(8,128)S(1)}, f32[128,128]{1,0:T(8,128)S(1)}, u32[]{:S(2)}, u32[]{:S(2)}) %collective-permute-start.1) | collective-permute-done | bytes 65568 | tf_op jit(solution)/shard_map/vx_second/ppermute | solution.py:540
  22.8 3.7 %send.1 = (f32[640,128]{1,0:T(8,128)}, f32[3,64,128]{2,1,0:T(8,128)S(1)}) custom-call(f32[4,16,128]{2,1,0:T(8,128)S(1)} %probe0.1.refs_0_, f32[4,24,128]{2,1,0:T(8,128)S(1)} %probe1.1.refs_1_, f32[4,24,128]{2,1,0:T(8,128)S(1)} %probe2.1.refs_2_, s32[64,128]{1,0:T(8,128)S(1)} %get-tuple-element.42.refs_3_.rank_ref, s32[64,128]{1,0:T(8,128)S(1)} %bitcast.30, ...), custom_call_target="tpu_custom_call" | custom-call | flops 3000000000 | bytes 9000000 | tf_op jit(solution)/shard_map/send/pallas_call | solution.py:522
  26.5 4.9 %all-to-all-start = ((f32[32,1,2560]{2,1,0:T(1,128)}), f32[32,1,2560]{2,1,0:T(1,128)S(1)}, u32[]{:S(2)}, u32[]{:S(2)}) async-start(f32[32,1,2560]{2,1,0:T(1,128)} %bitcast.8), calls=%async_computation | async-start | bytes 655360 | tf_op jit(solution)/shard_map/all_to_all | solution.py:596
  31.4 2.5 %flux.1 = (f32[256,8,128]{2,1,0:T(8,128)S(1)}, f32[128,128]{1,0:T(8,128)S(1)}, f32[128,128]{1,0:T(8,128)S(1)}, f32[8,128]{1,0:T(8,128)S(1)}, f32[8,128]{1,0:T(8,128)S(1)}) custom-call(f32[256,8,128]{2,1,0:T(8,128)S(1)} %get-tuple-element.45.v_ref, f32[128,128]{1,0:T(8,128)S(1)} %collective-permute-done.x1_ref, f32[128,128]{1,0:T(8,128)S(1)} %collective-permute-done.1.x2_ref, ...), custom_call_target="tpu_custom_call" | custom-call | flops 1000000000 | bytes 3000000 | tf_op jit(solution)/shard_map/flux/pallas_call | solution.py:522
  33.9 0.3 collective-permute-start.4
  34.2 1.4 %collective-permute-start.5 = (f32[128,128]{1,0:T(8,128)S(1)}, f32[128,128]{1,0:T(8,128)S(1)}, u32[]{:S(2)}, u32[]{:S(2)}) collective-permute-start(f32[128,128]{1,0:T(8,128)S(1)} %get-tuple-element.48), channel_id=1, source_target_pairs={{0,224},{32,64},{64,32},{96,128},{128,96},{160,192},{192,160},{224... | collective-permute-start | bytes 196616 | tf_op jit(solution)/shard_map/fx_second/ppermute | solution.py:540
  35.7 1.8 %collective-permute-start.6 = (f32[8,128]{1,0:T(8,128)S(1)}, f32[8,128]{1,0:T(8,128)S(1)}, u32[]{:S(2)}, u32[]{:S(2)}) collective-permute-start(f32[8,128]{1,0:T(8,128)S(1)} %get-tuple-element.49), channel_id=1, source_target_pairs={{0,1},{1,0},{2,3},{3,2},{4,5},{5,4},{6,7},{7,6},{8,9},{9,8},{10,11... | collective-permute-start | bytes 12296 | tf_op jit(solution)/shard_map/fz_first/ppermute | solution.py:538
  37.4 4.9 %collective-permute-start.7 = (f32[8,128]{1,0:T(8,128)S(1)}, f32[8,128]{1,0:T(8,128)S(1)}, u32[]{:S(2)}, u32[]{:S(2)}) collective-permute-start(f32[8,128]{1,0:T(8,128)S(1)} %get-tuple-element.50), channel_id=1, source_target_pairs={{0,31},{1,2},{2,1},{3,4},{4,3},{5,6},{6,5},{7,8},{8,7},{9,10},{10,... | collective-permute-start | bytes 12296 | tf_op jit(solution)/shard_map/fz_second/ppermute | solution.py:540
  42.3 0.0 collective-permute-done.6.z1_ref
  42.3 2.6 %collective-permute-done.7.z2_ref = f32[8,128]{1,0:T(8,128)S(1)} collective-permute-done((f32[8,128]{1,0:T(8,128)S(1)}, f32[8,128]{1,0:T(8,128)S(1)}, u32[]{:S(2)}, u32[]{:S(2)}) %collective-permute-start.7) | collective-permute-done | bytes 4128 | tf_op jit(solution)/shard_map/fz_second/ppermute | solution.py:540
  44.9 1.0 %assemble.1 = (f32[2048,128]{1,0:T(8,128)}, f32[64,8,128]{2,1,0:T(8,128)S(1)}) custom-call(f32[256,8,128]{2,1,0:T(8,128)S(1)} %get-tuple-element.46.part_ref, f32[128,128]{1,0:T(8,128)S(1)} %collective-permute-done.4.x1_ref, f32[128,128]{1,0:T(8,128)S(1)} %collective-permute-done.5.x2_ref, f32[8,128]{1,0:T(8,128)S(1)} %collective-permute-done.6.z1_ref, ...), custom_call_target="tpu_custom_call" | custom-call | flops 1000000000 | bytes 3000000 | tf_op jit(solution)/shard_map/assemble/pallas_call | solution.py:522
  46.0 2.8 %final.1 = (f32[2048,128]{1,0:T(8,128)}, f32[320,128]{1,0:T(8,128)}) custom-call(f32[2048,128]{1,0:T(8,128)} %get-tuple-element.51.kept_ref, f32[64,8,128]{2,1,0:T(8,128)S(1)} %get-tuple-element.52.bottom_ref, f32[640,128]{1,0:T(8,128)S(1)} %bitcast.23, f32[3,64,128]{2,1,0:T(8,128)S(1)} %get-tuple-element.53.own_ref, ...), custom_call_target="tpu_custom_call", output_to_operand_aliasing={{0}: (0, {})} | custom-call | flops 1000000000 | bytes 3000000 | tf_op jit(solution)/shard_map/final/pallas_call | solution.py:522
  (13 shorter events, 0.0 us)
Async XLA Ops:
  0.6 4.2 %copy-start = (s32[3,8192]{1,0:T(4,128)S(1)}, s32[3,8192]{1,0:T(4,128)}, u32[]{:S(2)}) copy-start(s32[3,8192]{1,0:T(4,128)} %refs_2_.5) | copy-start | bytes 294916
  0.6 4.2 %copy-start.2 = (s32[8192]{0:T(1024)S(1)}, s32[8192]{0:T(1024)}, u32[]{:S(2)}) copy-start(s32[8192]{0:T(1024)} %param.6) | copy-start | bytes 98308
  2.3 19.9 %collective-permute-start = (f32[128,128]{1,0:T(8,128)S(1)}, f32[128,128]{1,0:T(8,128)S(1)}, u32[]{:S(2)}, u32[]{:S(2)}) collective-permute-start(f32[128,128]{1,0:T(8,128)S(1)} %get-tuple-element.35), channel_id=1, source_target_pairs={{0,32},{32,0},{64,96},{96,64},{128,160},{160,128},{192,224},{224,1... | collective-permute-start | bytes 196616 | tf_op jit(solution)/shard_map/vx_first/ppermute | solution.py:538
  2.4 0.8 %copy-start.3 = (s32[8192,1]{0,1:T(1,128)S(1)}, s32[8192,1]{0,1:T(1,128)}, u32[]{:S(2)}) copy-start(s32[8192,1]{0,1:T(1,128)} %param.8) | copy-start | bytes 98308
  6.8 15.3 %collective-permute-start.2 = (f32[8,128]{1,0:T(8,128)S(1)}, f32[8,128]{1,0:T(8,128)S(1)}, u32[]{:S(2)}, u32[]{:S(2)}) collective-permute-start(f32[8,128]{1,0:T(8,128)S(1)} %get-tuple-element.39), channel_id=1, source_target_pairs={{0,1},{1,0},{2,3},{3,2},{4,5},{5,4},{6,7},{7,6},{8,9},{9,8},{10,11... | collective-permute-start | bytes 12296 | tf_op jit(solution)/shard_map/vz_first/ppermute | solution.py:538
  11.8 10.3 %collective-permute-start.3 = (f32[8,128]{1,0:T(8,128)S(1)}, f32[8,128]{1,0:T(8,128)S(1)}, u32[]{:S(2)}, u32[]{:S(2)}) collective-permute-start(f32[8,128]{1,0:T(8,128)S(1)} %get-tuple-element.41), channel_id=1, source_target_pairs={{0,31},{1,2},{2,1},{3,4},{4,3},{5,6},{6,5},{7,8},{8,7},{9,10},{10,... | collective-permute-start | bytes 12296 | tf_op jit(solution)/shard_map/vz_second/ppermute | solution.py:540
  19.1 3.7 %copy-start.1 = (f32[20480]{0:T(1024)S(1)}, f32[20480]{0:T(1024)}, u32[]{:S(2)}) copy-start(f32[20480]{0:T(1024)} %param.9) | copy-start | bytes 245764
  19.1 3.7 %copy-start.4 = (s32[8192,1]{0,1:T(1,128)S(1)}, s32[8192,1]{0,1:T(1,128)}, u32[]{:S(2)}) copy-start(s32[8192,1]{0,1:T(1,128)} %param.8) | copy-start | bytes 98308
  19.1 3.7 %collective-permute-start.1 = (f32[128,128]{1,0:T(8,128)S(1)}, f32[128,128]{1,0:T(8,128)S(1)}, u32[]{:S(2)}, u32[]{:S(2)}) collective-permute-start(f32[128,128]{1,0:T(8,128)S(1)} %get-tuple-element.37), channel_id=1, source_target_pairs={{0,224},{32,64},{64,32},{96,128},{128,96},{160,192},{192,160},{224... | collective-permute-start | bytes 196616 | tf_op jit(solution)/shard_map/vx_second/ppermute | solution.py:540
  26.5 19.4 %all-to-all-start = ((f32[32,1,2560]{2,1,0:T(1,128)}), f32[32,1,2560]{2,1,0:T(1,128)S(1)}, u32[]{:S(2)}, u32[]{:S(2)}) async-start(f32[32,1,2560]{2,1,0:T(1,128)} %bitcast.8), calls=%async_computation | async-start | bytes 655360 | tf_op jit(solution)/shard_map/all_to_all | solution.py:596
  33.9 11.0 %collective-permute-start.4 = (f32[128,128]{1,0:T(8,128)S(1)}, f32[128,128]{1,0:T(8,128)S(1)}, u32[]{:S(2)}, u32[]{:S(2)}) collective-permute-start(f32[128,128]{1,0:T(8,128)S(1)} %get-tuple-element.47), channel_id=1, source_target_pairs={{0,32},{32,0},{64,96},{96,64},{128,160},{160,128},{192,224},{224,1... | collective-permute-start | bytes 196616 | tf_op jit(solution)/shard_map/fx_first/ppermute | solution.py:538
  34.2 10.7 %collective-permute-start.5 = (f32[128,128]{1,0:T(8,128)S(1)}, f32[128,128]{1,0:T(8,128)S(1)}, u32[]{:S(2)}, u32[]{:S(2)}) collective-permute-start(f32[128,128]{1,0:T(8,128)S(1)} %get-tuple-element.48), channel_id=1, source_target_pairs={{0,224},{32,64},{64,32},{96,128},{128,96},{160,192},{192,160},{224... | collective-permute-start | bytes 196616 | tf_op jit(solution)/shard_map/fx_second/ppermute | solution.py:540
  35.7 6.7 %collective-permute-start.6 = (f32[8,128]{1,0:T(8,128)S(1)}, f32[8,128]{1,0:T(8,128)S(1)}, u32[]{:S(2)}, u32[]{:S(2)}) collective-permute-start(f32[8,128]{1,0:T(8,128)S(1)} %get-tuple-element.49), channel_id=1, source_target_pairs={{0,1},{1,0},{2,3},{3,2},{4,5},{5,4},{6,7},{7,6},{8,9},{9,8},{10,11... | collective-permute-start | bytes 12296 | tf_op jit(solution)/shard_map/fz_first/ppermute | solution.py:538
  37.4 7.5 %collective-permute-start.7 = (f32[8,128]{1,0:T(8,128)S(1)}, f32[8,128]{1,0:T(8,128)S(1)}, u32[]{:S(2)}, u32[]{:S(2)}) collective-permute-start(f32[8,128]{1,0:T(8,128)S(1)} %get-tuple-element.50), channel_id=1, source_target_pairs={{0,31},{1,2},{2,1},{3,4},{4,3},{5,6},{6,5},{7,8},{8,7},{9,10},{10,... | collective-permute-start | bytes 12296 | tf_op jit(solution)/shard_map/fz_second/ppermute | solution.py:540

commit v3 on v2

--- a/solution.py
+++ b/solution.py
@@ -420,17 +420,17 @@
         parts += [high, values[f] - high]
 
     code = (rank_ref[...] // 256) * N_WALL + dest_ref[...]
-    code_ids = iota((96, 128), 0)
+    code_ids = iota((96, 128), 0).astype(jnp.int16)
+    zero = jnp.zeros((), BF16)
     total = jnp.zeros((576, 256), F32)
     per = SEND_BLOCK // 128
     for block in range(M_DEV // SEND_BLOCK):
         for i in range(per):
             r = block * per + i
-            match = code_ids == code[r : r + 1]
+            match = code_ids == jnp.broadcast_to(code[r : r + 1], (96, 128)).astype(jnp.int16)
             for part in range(6):
-                lhs_ref[pl.ds(96 * part, 96), pl.ds(128 * r, 128)] = jnp.where(
-                    match, parts[part][r : r + 1], 0.0
-                ).astype(BF16)
+                value = jnp.broadcast_to(parts[part][r : r + 1], (96, 128)).astype(BF16)
+                lhs_ref[pl.ds(96 * part, 96), pl.ds(128 * r, 128)] = jnp.where(match, value, zero)
         span = pl.ds(block * SEND_BLOCK, SEND_BLOCK)
         total = total + lax.dot_general(
             lhs_ref[:, span], hot_ref[:, span], (((1,), (1,)), ((), ())), preferred_element_type=F32

time: 49.2 us -> 48.9 us (level)
  no operation moved by 1% of the time
where the time goes in v3:
time: 48.9 us; the launch traced here: 48.7 us
  starting transfers between devices  22.6 us (46%)
  Pallas kernels  21.1 us (43%)
  waiting for transfers between devices  3.26 us (7%)
  between operations  0.94 us (2%)
  local copies, waits for them, and re-layouts  0.77 us (2%)
    pallas_call x9, Pallas kernels, call(): pl.pallas_call(kernel, out_shape=[jax.ShapeDtypeStruct(shape, dtype) for...  21.1 us
    ppermute x4, starting transfers between devices, exchange(): lax.ppermute(second, axis, [(i, (i - 1 + 2 * (i % 2)) % count) for i in r...  13.5 us
    all_to_all x1, starting transfers between devices, local(): lax.all_to_all(send.reshape(N_WALL, 1, CHUNK * 128), 'wall', 0, 0, tiled=...  4.92 us
    ppermute x4, starting transfers between devices, exchange(): lax.ppermute(first, axis, [(i, i + 1 - 2 * (i % 2)) for i in range(count)])  4.19 us
    ppermute x4, waiting for transfers between devices, exchange(): lax.ppermute(second, axis, [(i, (i - 1 + 2 * (i % 2)) % count) for i in r...  3.24 us
  transfers between devices with their start and end apart: 9, of which 2 were waited for; matrix products, arithmetic and copies ran while one was open for 0% of the time, Pallas kernels for 27%

profile of v3, /device:TPU:8, one launch (start us, length us, event | category | flops | bytes accessed | tf_op | source)
XLA Modules:
  0.0 48.7 jit_solution(2668506065447202247)
XLA Ops:
  0.6 1.6 %entropy.1 = (f32[256,8,128]{2,1,0:T(8,128)S(1)}, bf16[1536,256]{1,0:T(8,128)(2,1)S(1)}, f32[128,128]{1,0:T(8,128)S(1)}, f32[128,128]{1,0:T(8,128)S(1)}, f32[8,128]{1,0:T(8,128)S(1)}, /*index=5*/f32[8,128]{1,0:T(8,128)S(1)}) custom-call(f32[5,512,128]{2,1,0:T(8,128)} %bitcast.32), custom_call_target="tpu_custom_call" | custom-call | flops 1000000000 | bytes 3000000 | tf_op jit(solution)/shard_map/entropy/pallas_call | solution.py:522
  2.3 0.1 collective-permute-start
  2.4 0.0 copy-start.3
  2.4 0.7 %copy-done.3 = s32[8192,1]{0,1:T(1,128)S(1)} copy-done((s32[8192,1]{0,1:T(1,128)S(1)}, s32[8192,1]{0,1:T(1,128)}, u32[]{:S(2)}) %copy-start.3) | copy-done | bytes 32792
  3.1 1.6 %rank.1 = (s32[64,128]{1,0:T(8,128)S(1)}, bf16[256,8192]{1,0:T(8,128)(2,1)S(1)}) custom-call(s32[1,8192]{1,0:T(1,128)S(1)} %bitcast.29), custom_call_target="tpu_custom_call" | custom-call | flops 1000000000 | bytes 3000000 | tf_op jit(solution)/shard_map/rank/pallas_call | solution.py:522
  4.8 2.0 %probe0.1.refs_0_ = f32[4,16,128]{2,1,0:T(8,128)S(1)} custom-call(bf16[1536,256]{1,0:T(8,128)(2,1)S(1)} %get-tuple-element.34.refs_0_, s32[1,8192]{1,0:T(1,128)S(1)} %bitcast.26, s32[3,8192]{1,0:T(4,128)S(1)} %copy-done), custom_call_target="tpu_custom_call" | custom-call | flops 5000000000 | bytes 15000000 | tf_op jit(solution)/shard_map/probe0/pallas_call | solution.py:522
  6.8 2.0 %collective-permute-start.2 = (f32[8,128]{1,0:T(8,128)S(1)}, f32[8,128]{1,0:T(8,128)S(1)}, u32[]{:S(2)}, u32[]{:S(2)}) collective-permute-start(f32[8,128]{1,0:T(8,128)S(1)} %get-tuple-element.39), channel_id=1, source_target_pairs={{0,1},{1,0},{2,3},{3,2},{4,5},{5,4},{6,7},{7,6},{8,9},{9,8},{10,11... | collective-permute-start | bytes 12296 | tf_op jit(solution)/shard_map/vz_first/ppermute | solution.py:538
  8.8 3.0 %probe1.1.refs_1_ = f32[4,24,128]{2,1,0:T(8,128)S(1)} custom-call(bf16[1536,256]{1,0:T(8,128)(2,1)S(1)} %get-tuple-element.34.refs_0_, s32[1,8192]{1,0:T(1,128)S(1)} %bitcast.27, s32[3,8192]{1,0:T(4,128)S(1)} %copy-done), custom_call_target="tpu_custom_call" | custom-call | flops 5000000000 | bytes 15000000 | tf_op jit(solution)/shard_map/probe1/pallas_call | solution.py:522
  11.8 7.2 %collective-permute-start.3 = (f32[8,128]{1,0:T(8,128)S(1)}, f32[8,128]{1,0:T(8,128)S(1)}, u32[]{:S(2)}, u32[]{:S(2)}) collective-permute-start(f32[8,128]{1,0:T(8,128)S(1)} %get-tuple-element.41), channel_id=1, source_target_pairs={{0,31},{1,2},{2,1},{3,4},{4,3},{5,6},{6,5},{7,8},{8,7},{9,10},{10,... | collective-permute-start | bytes 12296 | tf_op jit(solution)/shard_map/vz_second/ppermute | solution.py:540
  19.1 0.0 collective-permute-start.1
  19.1 3.0 %probe2.1.refs_2_ = f32[4,24,128]{2,1,0:T(8,128)S(1)} custom-call(bf16[1536,256]{1,0:T(8,128)(2,1)S(1)} %get-tuple-element.34.refs_0_, s32[1,8192]{1,0:T(1,128)S(1)} %bitcast.28, s32[3,8192]{1,0:T(4,128)S(1)} %copy-done), custom_call_target="tpu_custom_call" | custom-call | flops 5000000000 | bytes 15000000 | tf_op jit(solution)/shard_map/probe2/pallas_call | solution.py:522
  22.1 0.0 collective-permute-done.2.z1_ref
  22.1 0.6 %collective-permute-done.1.x2_ref = f32[128,128]{1,0:T(8,128)S(1)} collective-permute-done((f32[128,128]{1,0:T(8,128)S(1)}, f32[128,128]{1,0:T(8,128)S(1)}, u32[]{:S(2)}, u32[]{:S(2)}) %collective-permute-start.1) | collective-permute-done | bytes 65568 | tf_op jit(solution)/shard_map/vx_second/ppermute | solution.py:540
  22.8 3.5 %send.1 = (f32[640,128]{1,0:T(8,128)}, f32[3,64,128]{2,1,0:T(8,128)S(1)}) custom-call(f32[4,16,128]{2,1,0:T(8,128)S(1)} %probe0.1.refs_0_, f32[4,24,128]{2,1,0:T(8,128)S(1)} %probe1.1.refs_1_, f32[4,24,128]{2,1,0:T(8,128)S(1)} %probe2.1.refs_2_, s32[64,128]{1,0:T(8,128)S(1)} %get-tuple-element.42.refs_3_.rank_ref, s32[64,128]{1,0:T(8,128)S(1)} %bitcast.30, ...), custom_call_target="tpu_custom_call" | custom-call | flops 3000000000 | bytes 9000000 | tf_op jit(solution)/shard_map/send/pallas_call | solution.py:522
  26.3 4.9 %all-to-all-start = ((f32[32,1,2560]{2,1,0:T(1,128)}), f32[32,1,2560]{2,1,0:T(1,128)S(1)}, u32[]{:S(2)}, u32[]{:S(2)}) async-start(f32[32,1,2560]{2,1,0:T(1,128)} %bitcast.8), calls=%async_computation | async-start | bytes 655360 | tf_op jit(solution)/shard_map/all_to_all | solution.py:596
  31.2 2.5 %flux.1 = (f32[256,8,128]{2,1,0:T(8,128)S(1)}, f32[128,128]{1,0:T(8,128)S(1)}, f32[128,128]{1,0:T(8,128)S(1)}, f32[8,128]{1,0:T(8,128)S(1)}, f32[8,128]{1,0:T(8,128)S(1)}) custom-call(f32[256,8,128]{2,1,0:T(8,128)S(1)} %get-tuple-element.45.v_ref, f32[128,128]{1,0:T(8,128)S(1)} %collective-permute-done.x1_ref, f32[128,128]{1,0:T(8,128)S(1)} %collective-permute-done.1.x2_ref, ...), custom_call_target="tpu_custom_call" | custom-call | flops 1000000000 | bytes 3000000 | tf_op jit(solution)/shard_map/flux/pallas_call | solution.py:522
  33.7 0.3 collective-permute-start.4
  34.0 1.4 %collective-permute-start.5 = (f32[128,128]{1,0:T(8,128)S(1)}, f32[128,128]{1,0:T(8,128)S(1)}, u32[]{:S(2)}, u32[]{:S(2)}) collective-permute-start(f32[128,128]{1,0:T(8,128)S(1)} %get-tuple-element.48), channel_id=1, source_target_pairs={{0,224},{32,64},{64,32},{96,128},{128,96},{160,192},{192,160},{224... | collective-permute-start | bytes 196616 | tf_op jit(solution)/shard_map/fx_second/ppermute | solution.py:540
  35.4 1.8 %collective-permute-start.6 = (f32[8,128]{1,0:T(8,128)S(1)}, f32[8,128]{1,0:T(8,128)S(1)}, u32[]{:S(2)}, u32[]{:S(2)}) collective-permute-start(f32[8,128]{1,0:T(8,128)S(1)} %get-tuple-element.49), channel_id=1, source_target_pairs={{0,1},{1,0},{2,3},{3,2},{4,5},{5,4},{6,7},{7,6},{8,9},{9,8},{10,11... | collective-permute-start | bytes 12296 | tf_op jit(solution)/shard_map/fz_first/ppermute | solution.py:538
  37.2 4.9 %collective-permute-start.7 = (f32[8,128]{1,0:T(8,128)S(1)}, f32[8,128]{1,0:T(8,128)S(1)}, u32[]{:S(2)}, u32[]{:S(2)}) collective-permute-start(f32[8,128]{1,0:T(8,128)S(1)} %get-tuple-element.50), channel_id=1, source_target_pairs={{0,31},{1,2},{2,1},{3,4},{4,3},{5,6},{6,5},{7,8},{8,7},{9,10},{10,... | collective-permute-start | bytes 12296 | tf_op jit(solution)/shard_map/fz_second/ppermute | solution.py:540
  42.1 0.0 collective-permute-done.6.z1_ref
  42.1 2.6 %collective-permute-done.7.z2_ref = f32[8,128]{1,0:T(8,128)S(1)} collective-permute-done((f32[8,128]{1,0:T(8,128)S(1)}, f32[8,128]{1,0:T(8,128)S(1)}, u32[]{:S(2)}, u32[]{:S(2)}) %collective-permute-start.7) | collective-permute-done | bytes 4128 | tf_op jit(solution)/shard_map/fz_second/ppermute | solution.py:540
  44.7 1.0 %assemble.1 = (f32[2048,128]{1,0:T(8,128)}, f32[64,8,128]{2,1,0:T(8,128)S(1)}) custom-call(f32[256,8,128]{2,1,0:T(8,128)S(1)} %get-tuple-element.46.part_ref, f32[128,128]{1,0:T(8,128)S(1)} %collective-permute-done.4.x1_ref, f32[128,128]{1,0:T(8,128)S(1)} %collective-permute-done.5.x2_ref, f32[8,128]{1,0:T(8,128)S(1)} %collective-permute-done.6.z1_ref, ...), custom_call_target="tpu_custom_call" | custom-call | flops 1000000000 | bytes 3000000 | tf_op jit(solution)/shard_map/assemble/pallas_call | solution.py:522
  45.7 2.8 %final.1 = (f32[2048,128]{1,0:T(8,128)}, f32[320,128]{1,0:T(8,128)}) custom-call(f32[2048,128]{1,0:T(8,128)} %get-tuple-element.51.kept_ref, f32[64,8,128]{2,1,0:T(8,128)S(1)} %get-tuple-element.52.bottom_ref, f32[640,128]{1,0:T(8,128)S(1)} %bitcast.23, f32[3,64,128]{2,1,0:T(8,128)S(1)} %get-tuple-element.53.own_ref, ...), custom_call_target="tpu_custom_call", output_to_operand_aliasing={{0}: (0, {})} | custom-call | flops 1000000000 | bytes 3000000 | tf_op jit(solution)/shard_map/final/pallas_call | solution.py:522
  (13 shorter events, 0.0 us)
Async XLA Ops:
  0.6 4.2 %copy-start = (s32[3,8192]{1,0:T(4,128)S(1)}, s32[3,8192]{1,0:T(4,128)}, u32[]{:S(2)}) copy-start(s32[3,8192]{1,0:T(4,128)} %refs_2_.5) | copy-start | bytes 294916
  0.6 4.2 %copy-start.2 = (s32[8192]{0:T(1024)S(1)}, s32[8192]{0:T(1024)}, u32[]{:S(2)}) copy-start(s32[8192]{0:T(1024)} %param.6) | copy-start | bytes 98308
  2.3 19.9 %collective-permute-start = (f32[128,128]{1,0:T(8,128)S(1)}, f32[128,128]{1,0:T(8,128)S(1)}, u32[]{:S(2)}, u32[]{:S(2)}) collective-permute-start(f32[128,128]{1,0:T(8,128)S(1)} %get-tuple-element.35), channel_id=1, source_target_pairs={{0,32},{32,0},{64,96},{96,64},{128,160},{160,128},{192,224},{224,1... | collective-permute-start | bytes 196616 | tf_op jit(solution)/shard_map/vx_first/ppermute | solution.py:538
  2.4 0.8 %copy-start.3 = (s32[8192,1]{0,1:T(1,128)S(1)}, s32[8192,1]{0,1:T(1,128)}, u32[]{:S(2)}) copy-start(s32[8192,1]{0,1:T(1,128)} %param.8) | copy-start | bytes 98308
  6.8 15.3 %collective-permute-start.2 = (f32[8,128]{1,0:T(8,128)S(1)}, f32[8,128]{1,0:T(8,128)S(1)}, u32[]{:S(2)}, u32[]{:S(2)}) collective-permute-start(f32[8,128]{1,0:T(8,128)S(1)} %get-tuple-element.39), channel_id=1, source_target_pairs={{0,1},{1,0},{2,3},{3,2},{4,5},{5,4},{6,7},{7,6},{8,9},{9,8},{10,11... | collective-permute-start | bytes 12296 | tf_op jit(solution)/shard_map/vz_first/ppermute | solution.py:538
  11.8 10.3 %collective-permute-start.3 = (f32[8,128]{1,0:T(8,128)S(1)}, f32[8,128]{1,0:T(8,128)S(1)}, u32[]{:S(2)}, u32[]{:S(2)}) collective-permute-start(f32[8,128]{1,0:T(8,128)S(1)} %get-tuple-element.41), channel_id=1, source_target_pairs={{0,31},{1,2},{2,1},{3,4},{4,3},{5,6},{6,5},{7,8},{8,7},{9,10},{10,... | collective-permute-start | bytes 12296 | tf_op jit(solution)/shard_map/vz_second/ppermute | solution.py:540
  19.1 3.7 %copy-start.1 = (f32[20480]{0:T(1024)S(1)}, f32[20480]{0:T(1024)}, u32[]{:S(2)}) copy-start(f32[20480]{0:T(1024)} %param.9) | copy-start | bytes 245764
  19.1 3.7 %copy-start.4 = (s32[8192,1]{0,1:T(1,128)S(1)}, s32[8192,1]{0,1:T(1,128)}, u32[]{:S(2)}) copy-start(s32[8192,1]{0,1:T(1,128)} %param.8) | copy-start | bytes 98308
  19.1 3.7 %collective-permute-start.1 = (f32[128,128]{1,0:T(8,128)S(1)}, f32[128,128]{1,0:T(8,128)S(1)}, u32[]{:S(2)}, u32[]{:S(2)}) collective-permute-start(f32[128,128]{1,0:T(8,128)S(1)} %get-tuple-element.37), channel_id=1, source_target_pairs={{0,224},{32,64},{64,32},{96,128},{128,96},{160,192},{192,160},{224... | collective-permute-start | bytes 196616 | tf_op jit(solution)/shard_map/vx_second/ppermute | solution.py:540
  26.3 19.5 %all-to-all-start = ((f32[32,1,2560]{2,1,0:T(1,128)}), f32[32,1,2560]{2,1,0:T(1,128)S(1)}, u32[]{:S(2)}, u32[]{:S(2)}) async-start(f32[32,1,2560]{2,1,0:T(1,128)} %bitcast.8), calls=%async_computation | async-start | bytes 655360 | tf_op jit(solution)/shard_map/all_to_all | solution.py:596
  33.7 11.0 %collective-permute-start.4 = (f32[128,128]{1,0:T(8,128)S(1)}, f32[128,128]{1,0:T(8,128)S(1)}, u32[]{:S(2)}, u32[]{:S(2)}) collective-permute-start(f32[128,128]{1,0:T(8,128)S(1)} %get-tuple-element.47), channel_id=1, source_target_pairs={{0,32},{32,0},{64,96},{96,64},{128,160},{160,128},{192,224},{224,1... | collective-permute-start | bytes 196616 | tf_op jit(solution)/shard_map/fx_first/ppermute | solution.py:538
  34.0 10.7 %collective-permute-start.5 = (f32[128,128]{1,0:T(8,128)S(1)}, f32[128,128]{1,0:T(8,128)S(1)}, u32[]{:S(2)}, u32[]{:S(2)}) collective-permute-start(f32[128,128]{1,0:T(8,128)S(1)} %get-tuple-element.48), channel_id=1, source_target_pairs={{0,224},{32,64},{64,32},{96,128},{128,96},{160,192},{192,160},{224... | collective-permute-start | bytes 196616 | tf_op jit(solution)/shard_map/fx_second/ppermute | solution.py:540
  35.4 6.7 %collective-permute-start.6 = (f32[8,128]{1,0:T(8,128)S(1)}, f32[8,128]{1,0:T(8,128)S(1)}, u32[]{:S(2)}, u32[]{:S(2)}) collective-permute-start(f32[8,128]{1,0:T(8,128)S(1)} %get-tuple-element.49), channel_id=1, source_target_pairs={{0,1},{1,0},{2,3},{3,2},{4,5},{5,4},{6,7},{7,6},{8,9},{9,8},{10,11... | collective-permute-start | bytes 12296 | tf_op jit(solution)/shard_map/fz_first/ppermute | solution.py:538
  37.2 7.5 %collective-permute-start.7 = (f32[8,128]{1,0:T(8,128)S(1)}, f32[8,128]{1,0:T(8,128)S(1)}, u32[]{:S(2)}, u32[]{:S(2)}) collective-permute-start(f32[8,128]{1,0:T(8,128)S(1)} %get-tuple-element.50), channel_id=1, source_target_pairs={{0,31},{1,2},{2,1},{3,4},{4,3},{5,6},{6,5},{7,8},{8,7},{9,10},{10,... | collective-permute-start | bytes 12296 | tf_op jit(solution)/shard_map/fz_second/ppermute | solution.py:540
